TPU v7x, 512 devices: a whole 4x8x8 slice. The times are simulated.
512 devices in a mesh: dp: 64 (over y, x, core), space: 8 (over z).
Axes of the slice: x: 4, y: 8, z: 8, core: 2. Of those that a mesh axis runs over, the one named last changes fastest.
Arguments:
- image: bfloat16 [64, 32, 8, 8, 128], P('dp', 'space'), may hold values from -30 to 30
- cotangent: bfloat16 [64, 32, 8, 8, 128], P('dp', 'space'), may hold values from -30 to 30
- first_weight: bfloat16 [3456, 128], P('dp'), may hold values from -0.109375 to 0.109375
- second_weight: bfloat16 [3456, 128], P('dp'), may hold values from -0.109375 to 0.109375
Outputs:
- output: bfloat16 [64, 32, 8, 8, 128], P('dp', 'space')
- image_grad: bfloat16 [64, 32, 8, 8, 128], P('dp', 'space')
- first_grad: float32 [3456, 128], P('dp')
- second_grad: float32 [3456, 128], P('dp')
All inputs are finite; a program needn't handle non-finite values.
Results may differ from a plain program's by a relative error of at most 0.013.
Values may be sent and summed in bfloat16 or wider, within the bound.
No kernel may reach another device: no remote copies, remote signals or barrier semaphores. Data moves between devices by JAX's collectives and lax.ppermute only.
A program may use at most 64 MiB of HBM per device.

v0:
```python
import functools
import math

import jax
import jax.numpy as jnp
from jax import lax
from jax.experimental import pallas as pl
from jax.experimental.pallas import tpu as pltpu
from jax.sharding import Mesh, PartitionSpec as P


EPSILON = 1e-05
C = 128
H = 8
W = 8
PLANE = H * W
TAPS = 27
NINE = 9 * C
ROWS = TAPS * C
BLOCK = 128
STEP = 16
SPLIT = 8

bf16 = jnp.bfloat16
f32 = jnp.float32


def phi_parts(u):
    cdf = 0.5 * (1.0 + lax.erf(u * 0.7071067811865476))
    return cdf


def slope_of(u, cdf):
    return cdf + u * jnp.exp(-0.5 * u * u) * 0.3989422804014327


def put_w_shifts(value, out, row):
    rows = value.shape[0]
    x = value.reshape(rows // PLANE, H, W, C)
    w_at = lax.broadcasted_iota(jnp.int32, x.shape, 2)
    left = jnp.where(w_at >= 1, pltpu.roll(x, 1, axis=2), 0.0)
    right = jnp.where(w_at <= W - 2, pltpu.roll(x, W - 1, axis=2), 0.0)
    for c, y in enumerate((left, x, right)):
        out[pl.ds(row, rows), c * C : (c + 1) * C] = y.reshape(rows, C).astype(bf16)


def h_down(x):
    return jnp.concatenate([jnp.zeros_like(x[:, :1]), x[:, : H - 1]], axis=1)


def h_up(x):
    return jnp.concatenate([x[:, 1:], jnp.zeros_like(x[:, :1])], axis=1)


def put_h_shifts(value, out, row):
    rows = value.shape[0]
    x = value.reshape(rows // PLANE, H, W, C)
    for b, y in enumerate((h_up(x), x, h_down(x))):
        out[pl.ds(row, rows), b * C : (b + 1) * C] = y.reshape(rows, C).astype(bf16)


def conv_into(acc, source, weight, planes, step):
    rows = step * PLANE

    margin = 2 * PLANE

    def clear(i, _):
        at = pl.ds(pl.multiple_of(i * margin, margin), margin)
        acc[at, :] = jnp.zeros((margin, C), f32)
        return 0

    lax.fori_loop(0, (planes + 2) // 2, clear, 0)

    def one(i, _):
        row = pl.multiple_of(i * rows, rows)
        z = jnp.dot(source[pl.ds(row, rows), :], weight[...], preferred_element_type=f32)
        for a in range(3):
            x = [
                z[:, (3 * a + b) * C : (3 * a + b + 1) * C].reshape(step, H, W, C)
                for b in range(3)
            ]
            total = h_down(x[0]) + x[1] + h_up(x[2])
            at = pl.ds(pl.multiple_of(row + (2 - a) * PLANE, PLANE), rows)
            acc[at, :] += total.reshape(rows, C)
        return 0

    lax.fori_loop(0, planes // step, one, 0)


def by_taps(flat, weight):
    for k in range(TAPS):
        c, ab = k % 3, k // 3
        weight[c * C : (c + 1) * C, ab * C : (ab + 1) * C] = flat[
            k * C : (k + 1) * C, :
        ].astype(bf16)


def reverse_into(weight, out):
    for k in range(TAPS):
        c, ab = k % 3, k // 3
        block = weight[(2 - c) * C : (3 - c) * C, (8 - ab) * C : (9 - ab) * C]
        out[c * C : (c + 1) * C, ab * C : (ab + 1) * C] = block.T


def assemble(core, mine, theirs, flat, weight):
    chips = mine.shape[0]
    part = ROWS // (2 * chips)
    mine_first = core == 0
    for y in range(chips):
        one = mine[y].astype(f32)
        two = theirs[y].astype(f32)
        even = jnp.where(mine_first, one, two)[:part]
        odd = jnp.where(mine_first, two, one)[:part]
        flat[2 * y * part : (2 * y + 1) * part, :] = even
        flat[(2 * y + 1) * part : (2 * y + 2) * part, :] = odd
    by_taps(flat, weight)


def row_sum(x):
    return jnp.sum(x, axis=0, keepdims=True)


def turn_into(source, turned):
    many = 4

    def turn(i, _):
        for n in range(many):
            at = pl.multiple_of((i * many + n) * C, C)
            for c in range(3):
                block = source[pl.ds(at, C), c * C : (c + 1) * C]
                turned[c * C : (c + 1) * C, pl.ds(at, C)] = block.T
        return 0

    lax.fori_loop(0, source.shape[0] // (many * C), turn, 0)


def grad_into(turned, delta, cells, flat, out, place, top):
    def shifted(a, first, last):
        row = (2 - a) * PLANE
        return delta[row : row + cells, first * C : last * C]

    jobs = [([(a, 0), (a, 1)], lambda a=a: shifted(a, 0, 2)) for a in range(3)]
    jobs.append(
        ([(0, 2), (1, 2)], lambda: jnp.concatenate([shifted(0, 2, 3), shifted(1, 2, 3)], axis=1))
    )
    jobs.append(([(2, 2)], lambda: shifted(2, 2, 3)))
    for taps, side in jobs:
        total = jnp.dot(turned[...], side(), preferred_element_type=f32)
        for n, (a, b) in enumerate(taps):
            for c in range(3):
                row = (9 * a + 3 * b + c) * C
                flat[row : row + C, :] = total[c * C : (c + 1) * C, n * C : (n + 1) * C]
    near, far, tall, _ = out.shape
    part = ROWS // (near * far)
    tall = tall // 2
    base = place[0] * (-(-part // SPLIT))
    for j in range(near * far):
        chunk = flat[pl.ds(j * part + base, tall), :].astype(bf16)
        out[j % near, j // near, top : top + tall, :] = chunk


def blocks_of(cells, body, init, rows=BLOCK):
    def one(i, carry):
        return body(i, pl.multiple_of(i * rows, rows), carry)

    return lax.fori_loop(0, cells // rows, one, init)


def statistics(conv, cells):
    zero = jnp.zeros((1, C), f32)

    def one(i, row, sums):
        acc = conv[pl.ds(row + PLANE, 4 * BLOCK), :]
        return (sums[0] + row_sum(acc), sums[1] + row_sum(acc * acc))

    total, square = blocks_of(cells, one, (zero, zero), 4 * BLOCK)
    average = total / cells
    return average, lax.rsqrt(square / cells - average * average + EPSILON)


def main_kernel(offsets, place, *refs):
    blocks, refs = refs[: len(offsets)], refs[len(offsets) :]
    (
        mine, theirs,
        output, outer_out, delta_out, grads_out, weight_out,
        image, cotangent, first_delta, outer_slab, grads,
        mine1, theirs1, mine2, theirs2, weight1, weight2, turned_weight,
        image_three, three, delta_three, turned, normed, conv, outer, flat,
        image_sem, other_sem, weight_sem, out_sem,
    ) = refs
    cells = image.shape[0]
    planes = cells // PLANE
    slab = output.shape[0]
    count = cells // slab
    padded = mine1.shape[1]
    zero = jnp.zeros((1, C), f32)
    copy = pltpu.make_async_copy
    fields = ([], [])
    for n, ((offset, index), block) in enumerate(zip(offsets, blocks)):
        owner = lax.rem(place[0] + (offset + count), count)
        at = pl.ds(pl.multiple_of(owner * slab, slab), slab)
        row = 2 * index * slab
        fields[0].append(copy(block.at[row : row + slab], image.at[at], image_sem.at[n]))
        fields[1].append(
            copy(block.at[row + slab : row + 2 * slab], cotangent.at[at], other_sem.at[n])
        )
    weights = [
        copy(source.at[:, half * padded : (half + 1) * padded], target, weight_sem.at[n])
        for n, (source, half, target) in enumerate(
            ((mine, 0, mine1), (theirs, 0, theirs1), (mine, 1, mine2), (theirs, 1, theirs2))
        )
    ]
    for c in fields[0] + weights + fields[1]:
        c.start()
    edge = jnp.zeros((PLANE, 3 * C), bf16)
    delta_three[0:PLANE, :] = edge
    delta_three[cells + PLANE : cells + 2 * PLANE, :] = edge
    for c in fields[0]:
        c.wait()

    def shift_image(i, row, _):
        put_w_shifts(image[pl.ds(row, BLOCK), :].astype(f32), image_three, row)
        return 0

    blocks_of(cells, shift_image, 0)
    for c in weights[:2]:
        c.wait()
    assemble(place[1], mine1, theirs1, flat, weight1)
    weight_copy = copy(weight1, weight_out, out_sem.at[0])
    weight_copy.start()
    conv_into(conv, image_three, weight1, planes, STEP)
    average1, inverse1 = statistics(conv, cells)

    def norm_one(i, row, _):
        u = (conv[pl.ds(row + PLANE, BLOCK), :] - average1) * inverse1
        normed[pl.ds(row, BLOCK), :] = u
        put_w_shifts(u * phi_parts(u), three, row)
        return 0

    blocks_of(cells, norm_one, 0)
    for c in weights[2:]:
        c.wait()
    assemble(place[1], mine2, theirs2, flat, weight2)
    conv_into(conv, three, weight2, planes, STEP)
    average, inverse = statistics(conv, cells)
    turn_into(three, turned)
    for c in fields[1]:
        c.wait()
    parts = slab // BLOCK

    def norm_two(i, row, sums):
        at = pl.ds(row, BLOCK)
        n = (conv[pl.ds(row + PLANE, BLOCK), :] - average) * inverse
        conv[pl.ds(row + PLANE, BLOCK), :] = n
        u = image[at, :].astype(f32) + n
        cdf = phi_parts(u)
        grad = cotangent[at, :].astype(f32) * slope_of(u, cdf)
        outer[at, :] = grad

        @pl.when(lax.div(i, parts) == place[0])
        def _():
            inner = pl.ds(pl.multiple_of(lax.rem(i, parts) * BLOCK, BLOCK), BLOCK)
            output[inner, :] = (u * cdf).astype(bf16)
            outer_slab[inner, :] = grad

        return (sums[0] + row_sum(grad), sums[1] + row_sum(grad * n))

    plain, paired = blocks_of(cells, norm_two, (zero, zero))
    outer_copy = copy(outer_slab, outer_out, out_sem.at[1])
    outer_copy.start()
    plain = plain / cells
    paired = paired / cells

    def back_two(i, row, _):
        n = conv[pl.ds(row + PLANE, BLOCK), :]
        value = inverse * (outer[pl.ds(row, BLOCK), :] - plain - n * paired)
        put_w_shifts(value, three, row)
        put_h_shifts(value, delta_three, row + PLANE)
        return 0

    blocks_of(cells, back_two, 0)
    half = grads.shape[2] // 2
    grad_into(turned, delta_three, cells, flat, grads, place, half)

    reverse_into(weight2, turned_weight)
    conv_into(conv, three, turned_weight, planes, STEP)

    def inner_grad(i, row, sums):
        u = normed[pl.ds(row, BLOCK), :]
        grad = conv[pl.ds(row + PLANE, BLOCK), :] * slope_of(u, phi_parts(u))
        conv[pl.ds(row + PLANE, BLOCK), :] = grad
        return (sums[0] + row_sum(grad), sums[1] + row_sum(grad * u))

    plain1, paired1 = blocks_of(cells, inner_grad, (zero, zero))
    plain1 = plain1 / cells
    paired1 = paired1 / cells

    def back_one(i, row, _):
        at = pl.ds(row, BLOCK)
        grad = conv[pl.ds(row + PLANE, BLOCK), :]
        value = inverse1 * (grad - plain1 - normed[at, :] * paired1)
        first_delta[at, :] = value.astype(bf16)
        put_h_shifts(value, delta_three, row + PLANE)
        return 0

    blocks_of(cells, back_one, 0)
    delta_copy = copy(first_delta, delta_out, out_sem.at[2])
    delta_copy.start()
    turn_into(image_three, turned)
    grad_into(turned, delta_three, cells, flat, grads, place, 0)
    grads_copy = copy(grads, grads_out, out_sem.at[3])
    grads_copy.start()
    for c in (weight_copy, outer_copy, delta_copy, grads_copy):
        c.wait()


def fourth_kernel(place, delta, weight, outer_slab, grad, three, conv, turned_weight):
    slab = grad.shape[0]
    planes = slab // PLANE
    last = delta.shape[0] // PLANE
    reverse_into(weight, turned_weight)
    base = place[0] * planes
    for p in range(planes + 2):
        d = base + (p - 1)
        inside = jnp.logical_and(d >= 0, d < last)
        at = pl.multiple_of(jnp.clip(d, 0, last - 1) * PLANE, PLANE)
        x = delta[pl.ds(at, PLANE), :].astype(f32)
        put_w_shifts(jnp.where(inside, x, 0.0), three, p * PLANE)
    conv_into(conv, three, turned_weight, planes + 2, planes + 2)
    total = conv[2 * PLANE : 2 * PLANE + slab, :]
    grad[...] = (outer_slab[...] + total).astype(bf16)


SMEM = pl.BlockSpec(memory_space=pltpu.SMEM)
VMEM = pl.BlockSpec(memory_space=pltpu.VMEM)
HBM = pl.BlockSpec(memory_space=pltpu.HBM)


def call(kernel, outs, scratch, *args, mib=4, far_in=(), far_out=()):
    specs = [
        HBM if n in far_in else SMEM if a.dtype == jnp.int32 else VMEM
        for n, a in enumerate(args)
    ]
    args = [
        pltpu.with_memory_space_constraint(a, pltpu.HBM) if n in far_in else a
        for n, a in enumerate(args)
    ]
    return pl.pallas_call(
        kernel,
        out_shape=tuple(jax.ShapeDtypeStruct(s, d) for s, d in outs),
        in_specs=specs,
        out_specs=tuple(HBM if n in far_out else VMEM for n in range(len(outs))),
        scratch_shapes=scratch,
        compiler_params=pltpu.CompilerParams(vmem_limit_bytes=mib * 1024 * 1024),
    )(*args)


def main_call(place, blocks, mine, theirs, slab, chunks):
    count = sum(len(offsets) for offsets, _ in blocks)
    cells = slab * count
    offsets = [(o, n) for many, _ in blocks for n, o in enumerate(many)]
    arrays = [array for many, array in blocks for _ in many]
    field = (cells, C)
    half = (mine.shape[0], mine.shape[1] // 2, C)
    local = pltpu.VMEM
    signal = pltpu.SemaphoreType.DMA
    return call(
        functools.partial(main_kernel, offsets),
        [
            ((slab, C), bf16), ((slab, C), f32), (field, bf16), (chunks, bf16),
            ((3 * C, NINE), bf16),
        ],
        [local(field, bf16)] * 3
        + [local((slab, C), f32), local(chunks, bf16)]
        + [local(half, bf16)] * 4
        + [local((3 * C, NINE), bf16)] * 3
        + [
            local((cells, 3 * C), bf16), local((cells, 3 * C), bf16),
            local((cells + 2 * PLANE, 3 * C), bf16), local((3 * C, cells), bf16),
            local(field, f32), local((cells + 2 * PLANE, C), f32), local(field, f32),
            local((ROWS + 8, C), f32),
            signal((count,)), signal((count,)), signal((4,)), signal((4,)),
        ],
        place, *arrays, mine, theirs,
        mib=32, far_in=range(1, count + 3), far_out=(1, 2, 3, 4),
    )


def fourth_call(place, delta, weight, outer_slab):
    slab = outer_slab.shape[0]
    return call(
        fourth_kernel,
        [((slab, C), bf16)],
        [
            pltpu.VMEM((slab + 2 * PLANE, 3 * C), bf16),
            pltpu.VMEM((slab + 4 * PLANE, C), f32),
            pltpu.VMEM((3 * C, NINE), bf16),
        ],
        place, delta, weight, outer_slab, mib=8,
    )[0]


def near_kernel(parts, out):
    out[...] = jnp.sum(parts[...].astype(f32), axis=0).astype(bf16)


def near_call(parts):
    return call(near_kernel, [(parts.shape[1:], bf16)], [], parts)[0]


def far_kernel(factor, parts, first, second):
    _, split, both, _ = parts.shape
    tall = both // 2
    part = first.shape[0]
    piece = -(-part // split)
    for s in range(split):
        total = jnp.sum(parts[:, s].astype(f32), axis=0) * factor
        rows = min(piece, part - s * piece)
        first[s * piece : s * piece + rows, :] = total[:rows]
        second[s * piece : s * piece + rows, :] = total[tall : tall + rows]


def far_call(parts, part, factor):
    return call(
        functools.partial(far_kernel, factor),
        [((part, C), f32), ((part, C), f32)], [], parts,
    )


def spread(x, axes, count):
    copies = jnp.broadcast_to(x[None], (count,) + x.shape)
    return lax.all_to_all(copies, axes, 0, 0, tiled=True)


def solution(mesh):
    dp, space = mesh.shape["dp"], mesh.shape["space"]
    across = 4
    fine = Mesh(
        mesh.devices.reshape(dp // (2 * across), across, 2, space),
        ("y", "x", "core", "space"),
    )
    chips = dp // 2
    swap = [(0, 1), (1, 0)]
    near = 2 * across
    far = dp // near

    def shifted(x, hops):
        pairs = [((i + hops) % space, i) for i in range(space)]
        return lax.ppermute(x, "space", pairs)

    def whole_patch(x):
        blocks = [((0,), x)]
        up = down = x
        for hops in range(1, space // 2):
            up = shifted(up, 1)
            down = shifted(down, -1)
            blocks += [((hops,), up), ((-hops,), down)]
        return blocks + [((space // 2,), shifted(x, space // 2))]

    def step(image, cotangent, first_weight, second_weight):
        slab = image.shape[1] * PLANE
        cells = slab * space
        part = first_weight.shape[0]
        padded = -(-part // 8) * 8
        piece = -(-part // space)
        chunks = (near, far, 2 * (-(-piece // 8) * 8), C)
        factor = 1.0 / math.sqrt(cells * dp)
        core = lax.axis_index("core")
        place = jnp.stack([lax.axis_index("space"), core]).astype(jnp.int32)

        tall = ((0, padded - part), (0, 0))
        shard = jnp.concatenate([jnp.pad(first_weight, tall), jnp.pad(second_weight, tall)])
        mine = spread(shard, ("y", "x"), chips)
        pair = jnp.concatenate([image.reshape(slab, C), cotangent.reshape(slab, C)])
        blocks = whole_patch(pair)
        theirs = lax.ppermute(mine, "core", swap)
        output, outer_slab, first_delta, grads, w1 = main_call(
            place, blocks, mine, theirs, slab, chunks
        )
        parts = lax.all_to_all(grads, ("x", "core"), 0, 0, tiled=True)
        image_grad = fourth_call(place, first_delta, w1, outer_slab)
        sums = near_call(parts)
        spaced = jnp.broadcast_to(sums[:, None], (far, space) + sums.shape[1:])
        ends = lax.all_to_all(
            spaced.reshape((far * space,) + sums.shape[1:]), ("y", "space"), 0, 0, tiled=True
        )
        first_grad, second_grad = far_call(
            ends.reshape((far, space) + sums.shape[1:]), part, factor
        )
        return (
            output.reshape(image.shape),
            image_grad.reshape(image.shape),
            first_grad,
            second_grad,
        )

    dp_axes = ("y", "x", "core")
    field = P(dp_axes, "space", None, None, None)
    rows = P(dp_axes, None)
    return jax.shard_map(
        step,
        mesh=fine,
        in_specs=(field, field, rows, rows),
        out_specs=(field, field, rows, rows),
        check_vma=False,
    )
```

profile of v0, /device:TPU:2, one launch (start us, length us, event | category | flops | bytes accessed | tf_op | source)
XLA Modules:
  0.0 133.1 jit_solution(13966958319066807805)
XLA Ops:
  0.6 0.7 fusion.2
  1.4 0.1 broadcast_in_dim.4
  1.5 0.0 copy-start.9
  1.5 0.0 copy-start.10
  1.5 35.4 %all_to_all.15.refs_8_ = bf16[32,112,128]{2,1,0:T(8,128)(2,1)S(1)} all-to-all(bf16[32,112,128]{2,1,0:T(8,128)(2,1)S(1)} %broadcast_in_dim.4), channel_id=1, replica_groups=mesh['y'=8,'x'=4,'core'=2,'space'=8] {'y','x'}, dimensions={0} | all-to-all | bytes 1835008 | tf_op jit(solution)/shard_map/all_to_all | solution.py:432
  37.0 0.0 copy-start
  37.0 1.9 %collective-permute-start.7 = (bf16[32,112,128]{2,1,0:T(8,128)(2,1)S(1)}, bf16[32,112,128]{2,1,0:T(8,128)(2,1)}, u32[]{:S(2)}, u32[]{:S(2)}) collective-permute-start(bf16[32,112,128]{2,1,0:T(8,128)(2,1)S(1)} %all_to_all.15.refs_8_), channel_id=1, source_target_pairs={{0,8},{8,0},{1,9},{9,1},{2,10},{10,2},{3,11},{11,3},{4,12},{12,4},... | collective-permute-start | bytes 2752520 | tf_op jit(solution)/shard_map/ppermute | solution.py:476
  38.9 0.0 copy-done.9
  38.9 0.0 copy-done.10
  38.9 0.0 copy-start.1
  38.9 4.3 %collective-permute-start.1 = (bf16[512,128]{1,0:T(8,128)(2,1)S(1)}, bf16[512,128]{1,0:T(8,128)(2,1)S(1)}, u32[]{:S(2)}, u32[]{:S(2)}) collective-permute-start(bf16[512,128]{1,0:T(8,128)(2,1)S(1)} %pad_maximum_fusion.refs_0_), channel_id=1, source_target_pairs={{7,0},{0,1},{1,2},{2,3},{3,4},{4,5},{5,6},{6,7},{15,8},{8,9},{9,10... | collective-permute-start | bytes 393224 | tf_op jit(solution)/shard_map/ppermute | solution.py:449
  43.2 8.6 %collective-permute-start = (bf16[512,128]{1,0:T(8,128)(2,1)S(1)}, bf16[512,128]{1,0:T(8,128)(2,1)S(1)}, u32[]{:S(2)}, u32[]{:S(2)}) collective-permute-start(bf16[512,128]{1,0:T(8,128)(2,1)S(1)} %pad_maximum_fusion.refs_0_), channel_id=1, source_target_pairs={{1,0},{2,1},{3,2},{4,3},{5,4},{6,5},{7,6},{0,7},{9,8},{10,9},{11,1... | collective-permute-start | bytes 393224 | tf_op jit(solution)/shard_map/ppermute | solution.py:449
  51.8 2.2 %collective-permute-done.1.refs_2_ = bf16[512,128]{1,0:T(8,128)(2,1)S(1)} collective-permute-done((bf16[512,128]{1,0:T(8,128)(2,1)S(1)}, bf16[512,128]{1,0:T(8,128)(2,1)S(1)}, u32[]{:S(2)}, u32[]{:S(2)}) %collective-permute-start.1) | collective-permute-done | bytes 131104 | tf_op jit(solution)/shard_map/ppermute | solution.py:449
  54.0 0.0 copy-start.2
  54.0 1.9 %collective-permute-start.3 = (bf16[512,128]{1,0:T(8,128)(2,1)S(1)}, bf16[512,128]{1,0:T(8,128)(2,1)S(1)}, u32[]{:S(2)}, u32[]{:S(2)}) collective-permute-start(bf16[512,128]{1,0:T(8,128)(2,1)S(1)} %collective-permute-done.1.refs_2_), channel_id=1, source_target_pairs={{7,0},{0,1},{1,2},{2,3},{3,4},{4,5},{5,6},{6,7},{15,8},{8,9},{9,10... | collective-permute-start | bytes 393224 | tf_op jit(solution)/shard_map/ppermute | solution.py:449
  55.9 0.0 collective-permute-done.refs_1_
  56.0 0.0 copy-start.3
  56.0 5.1 %collective-permute-start.2 = (bf16[512,128]{1,0:T(8,128)(2,1)S(1)}, bf16[512,128]{1,0:T(8,128)(2,1)S(1)}, u32[]{:S(2)}, u32[]{:S(2)}) collective-permute-start(bf16[512,128]{1,0:T(8,128)(2,1)S(1)} %collective-permute-done.refs_1_), channel_id=1, source_target_pairs={{1,0},{2,1},{3,2},{4,3},{5,4},{6,5},{7,6},{0,7},{9,8},{10,9},{11,1... | collective-permute-start | bytes 393224 | tf_op jit(solution)/shard_map/ppermute | solution.py:449
  61.1 4.8 %collective-permute-start.6 = (bf16[512,128]{1,0:T(8,128)(2,1)S(1)}, bf16[512,128]{1,0:T(8,128)(2,1)S(1)}, u32[]{:S(2)}, u32[]{:S(2)}) collective-permute-start(bf16[512,128]{1,0:T(8,128)(2,1)S(1)} %pad_maximum_fusion.refs_0_), channel_id=1, source_target_pairs={{4,0},{5,1},{6,2},{7,3},{0,4},{1,5},{2,6},{3,7},{12,8},{13,9},{14,... | collective-permute-start | bytes 393224 | tf_op jit(solution)/shard_map/ppermute | solution.py:449
  65.9 0.0 collective-permute-done.3.refs_4_
  65.9 0.0 copy-start.4
  66.0 1.9 %collective-permute-start.5 = (bf16[512,128]{1,0:T(8,128)(2,1)S(1)}, bf16[512,128]{1,0:T(8,128)(2,1)S(1)}, u32[]{:S(2)}, u32[]{:S(2)}) collective-permute-start(bf16[512,128]{1,0:T(8,128)(2,1)S(1)} %collective-permute-done.3.refs_4_), channel_id=1, source_target_pairs={{7,0},{0,1},{1,2},{2,3},{3,4},{4,5},{5,6},{6,7},{15,8},{8,9},{9,10... | collective-permute-start | bytes 393224 | tf_op jit(solution)/shard_map/ppermute | solution.py:449
  67.9 0.0 collective-permute-done.2.refs_3_
  67.9 0.0 copy-start.5
  67.9 5.1 %collective-permute-start.4 = (bf16[512,128]{1,0:T(8,128)(2,1)S(1)}, bf16[512,128]{1,0:T(8,128)(2,1)S(1)}, u32[]{:S(2)}, u32[]{:S(2)}) collective-permute-start(bf16[512,128]{1,0:T(8,128)(2,1)S(1)} %collective-permute-done.2.refs_3_), channel_id=1, source_target_pairs={{1,0},{2,1},{3,2},{4,3},{5,4},{6,5},{7,6},{0,7},{9,8},{10,9},{11,1... | collective-permute-start | bytes 393224 | tf_op jit(solution)/shard_map/ppermute | solution.py:449
  73.0 0.1 pad_add_fusion.place
  73.1 1.5 %collective-permute-done.6.refs_7_ = bf16[512,128]{1,0:T(8,128)(2,1)S(1)} collective-permute-done((bf16[512,128]{1,0:T(8,128)(2,1)S(1)}, bf16[512,128]{1,0:T(8,128)(2,1)S(1)}, u32[]{:S(2)}, u32[]{:S(2)}) %collective-permute-start.6) | collective-permute-done | bytes 131104 | tf_op jit(solution)/shard_map/ppermute | solution.py:449
  74.7 0.0 copy-start.6
  74.7 1.1 collective-permute-done.5.refs_6_
  75.7 0.0 copy-start.7
  75.7 0.0 collective-permute-done.4.refs_5_
  75.8 0.0 copy-start.8
  75.8 0.0 collective-permute-done.7.refs_9_
  75.8 0.0 copy-done
  75.8 0.0 copy-done.1
  75.8 0.0 copy-done.2
  75.8 0.0 copy-done.3
  75.8 0.0 copy-done.4
  75.8 0.0 copy-done.5
  75.8 0.0 copy-done.6
  75.8 0.6 copy-done.7
  76.4 0.1 copy-done.8
  76.5 23.3 %shard_map.75 = (bf16[256,128]{1,0:T(8,128)(2,1)}, f32[256,128]{1,0:T(8,128)S(1)}, bf16[2048,128]{1,0:T(8,128)(2,1)S(1)}, bf16[8,8,16,128]{3,2,1,0:T(8,128)(2,1)S(1)}, bf16[384,1152]{1,0:T(8,128)(2,1)S(1)}) custom-call(s32[2]{0:T(128)S(1)} %pad_add_fusion.place, bf16[512,128]{1,0:T(8,128)(2,1)} %copy-done.1, bf16[512,128]{1,0:T(8,128)(2,1)} %copy-done.3, ...), custom_call_target="tpu_custom_call" | custom-call | tf_op jit(solution)/shard_map/pallas_call | solution.py:348
  99.8 10.7 %all_to_all.16.parts = bf16[8,8,16,128]{3,2,1,0:T(8,128)(2,1)S(1)} all-to-all(bf16[8,8,16,128]{3,2,1,0:T(8,128)(2,1)S(1)} %get-tuple-element.15), channel_id=1, replica_groups=mesh['y'=8,'x'=4,'core'=2,'space'=8] {'x','core'}, dimensions={0} | all-to-all | bytes 524288 | tf_op jit(solution)/shard_map/all_to_all | solution.py:480
  110.5 0.7 broadcast_in_dim.5
  111.2 6.6 %all-to-all-start.2 = ((bf16[64,16,128]{2,1,0:T(8,128)(2,1)}), bf16[64,16,128]{2,1,0:T(8,128)(2,1)S(1)}, u32[]{:S(2)}, u32[]{:S(2)}) async-start(bf16[64,16,128]{2,1,0:T(8,128)(2,1)} %bitcast.6), calls=%async_computation.2 | async-start | bytes 524288 | tf_op jit(solution)/shard_map/all_to_all | solution.py:484
  117.8 2.1 %shard_map.76 = bf16[256,128]{1,0:T(8,128)(2,1)} custom-call(s32[2]{0:T(128)S(1)} %pad_add_fusion.place, bf16[2048,128]{1,0:T(8,128)(2,1)S(1)} %get-tuple-element.12.delta, bf16[384,1152]{1,0:T(8,128)(2,1)S(1)} %get-tuple-element.13.weight, f32[256,128]{1,0:T(8,128)S(1)} %get-tuple-element.14.outer_slab), custom_call_target="tpu_custom_call" | custom-call | tf_op jit(solution)/shard_map/pallas_call | solution.py:348
  120.0 12.5 %all-to-all-done.2 = bf16[64,16,128]{2,1,0:T(8,128)(2,1)S(1)} async-done(((bf16[64,16,128]{2,1,0:T(8,128)(2,1)}), bf16[64,16,128]{2,1,0:T(8,128)(2,1)S(1)}, u32[]{:S(2)}, u32[]{:S(2)}) %all-to-all-start.2) | async-done | bytes 262176 | tf_op jit(solution)/shard_map/all_to_all | solution.py:484
  132.4 0.7 shard_map.78
  (2 shorter events, 0.1 us)
Async XLA Ops:
  1.5 37.4 %copy-start.9 = (bf16[1,4,8,8,128]{4,3,2,1,0:T(8,128)(2,1)S(1)}, bf16[1,4,8,8,128]{4,3,2,1,0:T(8,128)(2,1)}, u32[]{:S(2)}) copy-start(bf16[1,4,8,8,128]{4,3,2,1,0:T(8,128)(2,1)} %param.5) | copy-start | bytes 196612
  1.5 37.4 %copy-start.10 = (bf16[1,4,8,8,128]{4,3,2,1,0:T(8,128)(2,1)S(1)}, bf16[1,4,8,8,128]{4,3,2,1,0:T(8,128)(2,1)}, u32[]{:S(2)}) copy-start(bf16[1,4,8,8,128]{4,3,2,1,0:T(8,128)(2,1)} %param.4) | copy-start | bytes 196612
  37.0 38.8 %copy-start = (bf16[32,112,128]{2,1,0:T(8,128)(2,1)}, bf16[32,112,128]{2,1,0:T(8,128)(2,1)S(1)}, u32[]{:S(2)}) copy-start(bf16[32,112,128]{2,1,0:T(8,128)(2,1)S(1)} %all_to_all.15.refs_8_) | copy-start | bytes 2752516
  37.0 38.8 %collective-permute-start.7 = (bf16[32,112,128]{2,1,0:T(8,128)(2,1)S(1)}, bf16[32,112,128]{2,1,0:T(8,128)(2,1)}, u32[]{:S(2)}, u32[]{:S(2)}) collective-permute-start(bf16[32,112,128]{2,1,0:T(8,128)(2,1)S(1)} %all_to_all.15.refs_8_), channel_id=1, source_target_pairs={{0,8},{8,0},{1,9},{9,1},{2,10},{10,2},{3,11},{11,3},{4,12},{12,4},... | collective-permute-start | bytes 2752520 | tf_op jit(solution)/shard_map/ppermute | solution.py:476
  38.9 36.9 %copy-start.1 = (bf16[512,128]{1,0:T(8,128)(2,1)}, bf16[512,128]{1,0:T(8,128)(2,1)S(1)}, u32[]{:S(2)}) copy-start(bf16[512,128]{1,0:T(8,128)(2,1)S(1)} %pad_maximum_fusion.refs_0_) | copy-start | bytes 393220
  38.9 15.1 %collective-permute-start.1 = (bf16[512,128]{1,0:T(8,128)(2,1)S(1)}, bf16[512,128]{1,0:T(8,128)(2,1)S(1)}, u32[]{:S(2)}, u32[]{:S(2)}) collective-permute-start(bf16[512,128]{1,0:T(8,128)(2,1)S(1)} %pad_maximum_fusion.refs_0_), channel_id=1, source_target_pairs={{7,0},{0,1},{1,2},{2,3},{3,4},{4,5},{5,6},{6,7},{15,8},{8,9},{9,10... | collective-permute-start | bytes 393224 | tf_op jit(solution)/shard_map/ppermute | solution.py:449
  43.2 12.7 %collective-permute-start = (bf16[512,128]{1,0:T(8,128)(2,1)S(1)}, bf16[512,128]{1,0:T(8,128)(2,1)S(1)}, u32[]{:S(2)}, u32[]{:S(2)}) collective-permute-start(bf16[512,128]{1,0:T(8,128)(2,1)S(1)} %pad_maximum_fusion.refs_0_), channel_id=1, source_target_pairs={{1,0},{2,1},{3,2},{4,3},{5,4},{6,5},{7,6},{0,7},{9,8},{10,9},{11,1... | collective-permute-start | bytes 393224 | tf_op jit(solution)/shard_map/ppermute | solution.py:449
  54.0 21.8 %copy-start.2 = (bf16[512,128]{1,0:T(8,128)(2,1)}, bf16[512,128]{1,0:T(8,128)(2,1)S(1)}, u32[]{:S(2)}) copy-start(bf16[512,128]{1,0:T(8,128)(2,1)S(1)} %collective-permute-done.1.refs_2_) | copy-start | bytes 393220
  54.0 11.9 %collective-permute-start.3 = (bf16[512,128]{1,0:T(8,128)(2,1)S(1)}, bf16[512,128]{1,0:T(8,128)(2,1)S(1)}, u32[]{:S(2)}, u32[]{:S(2)}) collective-permute-start(bf16[512,128]{1,0:T(8,128)(2,1)S(1)} %collective-permute-done.1.refs_2_), channel_id=1, source_target_pairs={{7,0},{0,1},{1,2},{2,3},{3,4},{4,5},{5,6},{6,7},{15,8},{8,9},{9,10... | collective-permute-start | bytes 393224 | tf_op jit(solution)/shard_map/ppermute | solution.py:449
  56.0 19.8 %copy-start.3 = (bf16[512,128]{1,0:T(8,128)(2,1)}, bf16[512,128]{1,0:T(8,128)(2,1)S(1)}, u32[]{:S(2)}) copy-start(bf16[512,128]{1,0:T(8,128)(2,1)S(1)} %collective-permute-done.refs_1_) | copy-start | bytes 393220
  56.0 11.9 %collective-permute-start.2 = (bf16[512,128]{1,0:T(8,128)(2,1)S(1)}, bf16[512,128]{1,0:T(8,128)(2,1)S(1)}, u32[]{:S(2)}, u32[]{:S(2)}) collective-permute-start(bf16[512,128]{1,0:T(8,128)(2,1)S(1)} %collective-permute-done.refs_1_), channel_id=1, source_target_pairs={{1,0},{2,1},{3,2},{4,3},{5,4},{6,5},{7,6},{0,7},{9,8},{10,9},{11,1... | collective-permute-start | bytes 393224 | tf_op jit(solution)/shard_map/ppermute | solution.py:449
  61.1 13.6 %collective-permute-start.6 = (bf16[512,128]{1,0:T(8,128)(2,1)S(1)}, bf16[512,128]{1,0:T(8,128)(2,1)S(1)}, u32[]{:S(2)}, u32[]{:S(2)}) collective-permute-start(bf16[512,128]{1,0:T(8,128)(2,1)S(1)} %pad_maximum_fusion.refs_0_), channel_id=1, source_target_pairs={{4,0},{5,1},{6,2},{7,3},{0,4},{1,5},{2,6},{3,7},{12,8},{13,9},{14,... | collective-permute-start | bytes 393224 | tf_op jit(solution)/shard_map/ppermute | solution.py:449
  65.9 9.9 %copy-start.4 = (bf16[512,128]{1,0:T(8,128)(2,1)}, bf16[512,128]{1,0:T(8,128)(2,1)S(1)}, u32[]{:S(2)}) copy-start(bf16[512,128]{1,0:T(8,128)(2,1)S(1)} %collective-permute-done.3.refs_4_) | copy-start | bytes 393220
  66.0 9.8 %collective-permute-start.5 = (bf16[512,128]{1,0:T(8,128)(2,1)S(1)}, bf16[512,128]{1,0:T(8,128)(2,1)S(1)}, u32[]{:S(2)}, u32[]{:S(2)}) collective-permute-start(bf16[512,128]{1,0:T(8,128)(2,1)S(1)} %collective-permute-done.3.refs_4_), channel_id=1, source_target_pairs={{7,0},{0,1},{1,2},{2,3},{3,4},{4,5},{5,6},{6,7},{15,8},{8,9},{9,10... | collective-permute-start | bytes 393224 | tf_op jit(solution)/shard_map/ppermute | solution.py:449
  67.9 7.9 %copy-start.5 = (bf16[512,128]{1,0:T(8,128)(2,1)}, bf16[512,128]{1,0:T(8,128)(2,1)S(1)}, u32[]{:S(2)}) copy-start(bf16[512,128]{1,0:T(8,128)(2,1)S(1)} %collective-permute-done.2.refs_3_) | copy-start | bytes 393220
  67.9 7.9 %collective-permute-start.4 = (bf16[512,128]{1,0:T(8,128)(2,1)S(1)}, bf16[512,128]{1,0:T(8,128)(2,1)S(1)}, u32[]{:S(2)}, u32[]{:S(2)}) collective-permute-start(bf16[512,128]{1,0:T(8,128)(2,1)S(1)} %collective-permute-done.2.refs_3_), channel_id=1, source_target_pairs={{1,0},{2,1},{3,2},{4,3},{5,4},{6,5},{7,6},{0,7},{9,8},{10,9},{11,1... | collective-permute-start | bytes 393224 | tf_op jit(solution)/shard_map/ppermute | solution.py:449
  74.7 1.2 copy-start.6
  75.7 0.7 copy-start.7
  75.8 0.7 copy-start.8
  111.2 21.2 %all-to-all-start.2 = ((bf16[64,16,128]{2,1,0:T(8,128)(2,1)}), bf16[64,16,128]{2,1,0:T(8,128)(2,1)S(1)}, u32[]{:S(2)}, u32[]{:S(2)}) async-start(bf16[64,16,128]{2,1,0:T(8,128)(2,1)} %bitcast.6), calls=%async_computation.2 | async-start | bytes 524288 | tf_op jit(solution)/shard_map/all_to_all | solution.py:484
where the time goes:
time: 134 us; the launch traced here: 133 us
  blocking collectives  46.1 us (34%)
  starting transfers between devices  40.3 us (30%)
  Pallas kernels  26.1 us (19%)
  waiting for transfers between devices  17.3 us (13%)
  local copies, waits for them, and re-layouts  1.52 us (1%)
    all_to_all x1, blocking collectives, spread(): return lax.all_to_all(copies, axes, 0, 0, tiled=True)  35.4 us
    ppermute x7, starting transfers between devices, shifted(): return lax.ppermute(x, 'space', pairs)  31.8 us
    pallas_call x4, Pallas kernels, call(): pl.pallas_call(kernel, out_shape=tuple((jax.ShapeDtypeStruct(s, d) for s,...  26.1 us
    all_to_all x1, waiting for transfers between devices, step(): lax.all_to_all(spaced.reshape((far * space,) + sums.shape[1:]), ('y', 'sp...  12.5 us
    all_to_all x1, blocking collectives, step(): parts = lax.all_to_all(grads, ('x', 'core'), 0, 0, tiled=True)  10.7 us
    all_to_all x1, starting transfers between devices, step(): lax.all_to_all(spaced.reshape((far * space,) + sums.shape[1:]), ('y', 'sp...  6.63 us
    ppermute x7, waiting for transfers between devices, shifted(): return lax.ppermute(x, 'space', pairs)  4.85 us
  transfers between devices with their start and end apart: 9, of which 4 were waited for; matrix products, arithmetic and copies ran while one was open for 0% of the time, Pallas kernels for 2%

commit v1 on v0

--- a/solution.py
+++ b/solution.py
@@ -59,7 +59,7 @@
         out[pl.ds(row, rows), b * C : (b + 1) * C] = y.reshape(rows, C).astype(bf16)
 
 
-def conv_into(acc, source, weight, planes, step):
+def conv_into(acc, source, weight, planes, step, turned=None):
     rows = step * PLANE
 
     margin = 2 * PLANE
@@ -82,6 +82,12 @@
             total = h_down(x[0]) + x[1] + h_up(x[2])
             at = pl.ds(pl.multiple_of(row + (2 - a) * PLANE, PLANE), rows)
             acc[at, :] += total.reshape(rows, C)
+        if turned is not None:
+            for n in range(rows // C):
+                at = pl.multiple_of(row + n * C, C)
+                for c in range(3):
+                    block = source[pl.ds(at, C), c * C : (c + 1) * C]
+                    turned[c * C : (c + 1) * C, pl.ds(at, C)] = block.T
         return 0
 
     lax.fori_loop(0, planes // step, one, 0)
@@ -103,12 +109,12 @@
 
 
 def assemble(core, mine, theirs, flat, weight):
-    chips = mine.shape[0]
+    across, chips = mine.shape[0], mine.shape[0] * mine.shape[1]
     part = ROWS // (2 * chips)
     mine_first = core == 0
     for y in range(chips):
-        one = mine[y].astype(f32)
-        two = theirs[y].astype(f32)
+        one = mine[y % across, y // across].astype(f32)
+        two = theirs[y % across, y // across].astype(f32)
         even = jnp.where(mine_first, one, two)[:part]
         odd = jnp.where(mine_first, two, one)[:part]
         flat[2 * y * part : (2 * y + 1) * part, :] = even
@@ -118,20 +124,6 @@
 
 def row_sum(x):
     return jnp.sum(x, axis=0, keepdims=True)
-
-
-def turn_into(source, turned):
-    many = 4
-
-    def turn(i, _):
-        for n in range(many):
-            at = pl.multiple_of((i * many + n) * C, C)
-            for c in range(3):
-                block = source[pl.ds(at, C), c * C : (c + 1) * C]
-                turned[c * C : (c + 1) * C, pl.ds(at, C)] = block.T
-        return 0
-
-    lax.fori_loop(0, source.shape[0] // (many * C), turn, 0)
 
 
 def grad_into(turned, delta, cells, flat, out, place, top):
@@ -185,14 +177,14 @@
         output, outer_out, delta_out, grads_out, weight_out,
         image, cotangent, first_delta, outer_slab, grads,
         mine1, theirs1, mine2, theirs2, weight1, weight2, turned_weight,
-        image_three, three, delta_three, turned, normed, conv, outer, flat,
+        image_three, three, delta_three, image_turned, turned, normed, conv, outer, flat,
         image_sem, other_sem, weight_sem, out_sem,
     ) = refs
     cells = image.shape[0]
     planes = cells // PLANE
     slab = output.shape[0]
     count = cells // slab
-    padded = mine1.shape[1]
+    padded = mine1.shape[2]
     zero = jnp.zeros((1, C), f32)
     copy = pltpu.make_async_copy
     fields = ([], [])
@@ -205,7 +197,7 @@
             copy(block.at[row + slab : row + 2 * slab], cotangent.at[at], other_sem.at[n])
         )
     weights = [
-        copy(source.at[:, half * padded : (half + 1) * padded], target, weight_sem.at[n])
+        copy(source.at[:, :, half * padded : (half + 1) * padded], target, weight_sem.at[n])
         for n, (source, half, target) in enumerate(
             ((mine, 0, mine1), (theirs, 0, theirs1), (mine, 1, mine2), (theirs, 1, theirs2))
         )
@@ -228,7 +220,7 @@
     assemble(place[1], mine1, theirs1, flat, weight1)
     weight_copy = copy(weight1, weight_out, out_sem.at[0])
     weight_copy.start()
-    conv_into(conv, image_three, weight1, planes, STEP)
+    conv_into(conv, image_three, weight1, planes, STEP, image_turned)
     average1, inverse1 = statistics(conv, cells)
 
     def norm_one(i, row, _):
@@ -241,9 +233,8 @@
     for c in weights[2:]:
         c.wait()
     assemble(place[1], mine2, theirs2, flat, weight2)
-    conv_into(conv, three, weight2, planes, STEP)
+    conv_into(conv, three, weight2, planes, STEP, turned)
     average, inverse = statistics(conv, cells)
-    turn_into(three, turned)
     for c in fields[1]:
         c.wait()
     parts = slab // BLOCK
@@ -306,8 +297,7 @@
     blocks_of(cells, back_one, 0)
     delta_copy = copy(first_delta, delta_out, out_sem.at[2])
     delta_copy.start()
-    turn_into(image_three, turned)
-    grad_into(turned, delta_three, cells, flat, grads, place, 0)
+    grad_into(image_turned, delta_three, cells, flat, grads, place, 0)
     grads_copy = copy(grads, grads_out, out_sem.at[3])
     grads_copy.start()
     for c in (weight_copy, outer_copy, delta_copy, grads_copy):
@@ -361,7 +351,7 @@
     offsets = [(o, n) for many, _ in blocks for n, o in enumerate(many)]
     arrays = [array for many, array in blocks for _ in many]
     field = (cells, C)
-    half = (mine.shape[0], mine.shape[1] // 2, C)
+    half = mine.shape[:2] + (mine.shape[2] // 2, C)
     local = pltpu.VMEM
     signal = pltpu.SemaphoreType.DMA
     return call(
@@ -376,7 +366,8 @@
         + [local((3 * C, NINE), bf16)] * 3
         + [
             local((cells, 3 * C), bf16), local((cells, 3 * C), bf16),
-            local((cells + 2 * PLANE, 3 * C), bf16), local((3 * C, cells), bf16),
+            local((cells + 2 * PLANE, 3 * C), bf16),
+            local((3 * C, cells), bf16), local((3 * C, cells), bf16),
             local(field, f32), local((cells + 2 * PLANE, C), f32), local(field, f32),
             local((ROWS + 8, C), f32),
             signal((count,)), signal((count,)), signal((4,)), signal((4,)),
@@ -439,7 +430,6 @@
         mesh.devices.reshape(dp // (2 * across), across, 2, space),
         ("y", "x", "core", "space"),
     )
-    chips = dp // 2
     swap = [(0, 1), (1, 0)]
     near = 2 * across
     far = dp // near
@@ -470,7 +460,8 @@
 
         tall = ((0, padded - part), (0, 0))
         shard = jnp.concatenate([jnp.pad(first_weight, tall), jnp.pad(second_weight, tall)])
-        mine = spread(shard, ("y", "x"), chips)
+        column = spread(shard, "y", far)
+        mine = spread(column, "x", across)
         pair = jnp.concatenate([image.reshape(slab, C), cotangent.reshape(slab, C)])
         blocks = whole_patch(pair)
         theirs = lax.ppermute(mine, "core", swap)

time: 134 us -> 130 us (0.970)
  blocking collectives: 46.1 us -> 43.3 us
    all_to_all x1 -> x2, blocking collectives: 35.4 us -> 33.4 us  [spread(): return lax.all_to_all(copies, axes, 0, 0, tiled=True)]
where the time goes in v1:
time: 130 us
  blocking collectives  43.3 us (33%)
  starting transfers between devices  40.8 us (31%)
  Pallas kernels  24.9 us (19%)
  waiting for transfers between devices  17.3 us (13%)
  local copies, waits for them, and re-layouts  1.55 us (1%)
    all_to_all x2, blocking collectives, spread(): return lax.all_to_all(copies, axes, 0, 0, tiled=True)  33.4 us
    ppermute x7, starting transfers between devices, shifted(): return lax.ppermute(x, 'space', pairs)  31.8 us
    pallas_call x4, Pallas kernels, call(): pl.pallas_call(kernel, out_shape=tuple((jax.ShapeDtypeStruct(s, d) for s,...  24.9 us
    all_to_all x1, waiting for transfers between devices, step(): lax.all_to_all(spaced.reshape((far * space,) + sums.shape[1:]), ('y', 'sp...  12.5 us
    all_to_all x1, blocking collectives, step(): parts = lax.all_to_all(grads, ('x', 'core'), 0, 0, tiled=True)  9.92 us
    all_to_all x1, starting transfers between devices, step(): lax.all_to_all(spaced.reshape((far * space,) + sums.shape[1:]), ('y', 'sp...  7.09 us
    ppermute x7, waiting for transfers between devices, shifted(): return lax.ppermute(x, 'space', pairs)  4.85 us
  transfers between devices with their start and end apart: 9, of which 4 were waited for; matrix products, arithmetic and copies ran while one was open for 0% of the time, Pallas kernels for 2%

profile of v1, /device:TPU:2, one launch (start us, length us, event | category | flops | bytes accessed | tf_op | source)
XLA Modules:
  0.0 129.6 jit_solution(11966812371203292370)
XLA Ops:
  0.6 0.7 fusion.2
  1.4 18.1 %all_to_all.20 = bf16[8,112,128]{2,1,0:T(8,128)(2,1)S(1)} all-to-all(bf16[8,112,128]{2,1,0:T(8,128)(2,1)S(1)} %broadcast_in_dim.6), channel_id=1, replica_groups=mesh['y'=8,'x'=4,'core'=2,'space'=8] {'y'}, dimensions={0} | all-to-all | bytes 458752 | tf_op jit(solution)/shard_map/all_to_all | solution.py:423
  19.5 0.1 broadcast_in_dim.7
  19.6 0.0 copy-start.9
  19.6 0.0 copy-start.10
  19.6 15.4 %all_to_all.21.refs_8_ = bf16[4,8,112,128]{3,2,1,0:T(8,128)(2,1)S(1)} all-to-all(bf16[4,8,112,128]{3,2,1,0:T(8,128)(2,1)S(1)} %broadcast_in_dim.7), channel_id=1, replica_groups=mesh['y'=8,'x'=4,'core'=2,'space'=8] {'x'}, dimensions={0} | all-to-all | bytes 1835008 | tf_op jit(solution)/shard_map/all_to_all | solution.py:423
  35.0 0.0 copy-start
  35.0 1.9 %collective-permute-start.7 = (bf16[4,8,112,128]{3,2,1,0:T(8,128)(2,1)S(1)}, bf16[4,8,112,128]{3,2,1,0:T(8,128)(2,1)}, u32[]{:S(2)}, u32[]{:S(2)}) collective-permute-start(bf16[4,8,112,128]{3,2,1,0:T(8,128)(2,1)S(1)} %all_to_all.21.refs_8_), channel_id=1, source_target_pairs={{0,8},{8,0},{1,9},{9,1},{2,10},{10,2},{3,11},{11,3},{4,12},{12,4},... | collective-permute-start | bytes 2752520 | tf_op jit(solution)/shard_map/ppermute | solution.py:467
  36.9 0.0 copy-done.9
  36.9 0.0 copy-done.10
  36.9 0.0 copy-start.1
  36.9 4.3 %collective-permute-start.1 = (bf16[512,128]{1,0:T(8,128)(2,1)S(1)}, bf16[512,128]{1,0:T(8,128)(2,1)S(1)}, u32[]{:S(2)}, u32[]{:S(2)}) collective-permute-start(bf16[512,128]{1,0:T(8,128)(2,1)S(1)} %pad_maximum_fusion.refs_0_), channel_id=1, source_target_pairs={{7,0},{0,1},{1,2},{2,3},{3,4},{4,5},{5,6},{6,7},{15,8},{8,9},{9,10... | collective-permute-start | bytes 393224 | tf_op jit(solution)/shard_map/ppermute | solution.py:439
  41.2 8.6 %collective-permute-start = (bf16[512,128]{1,0:T(8,128)(2,1)S(1)}, bf16[512,128]{1,0:T(8,128)(2,1)S(1)}, u32[]{:S(2)}, u32[]{:S(2)}) collective-permute-start(bf16[512,128]{1,0:T(8,128)(2,1)S(1)} %pad_maximum_fusion.refs_0_), channel_id=1, source_target_pairs={{1,0},{2,1},{3,2},{4,3},{5,4},{6,5},{7,6},{0,7},{9,8},{10,9},{11,1... | collective-permute-start | bytes 393224 | tf_op jit(solution)/shard_map/ppermute | solution.py:439
  49.8 2.2 %collective-permute-done.1.refs_2_ = bf16[512,128]{1,0:T(8,128)(2,1)S(1)} collective-permute-done((bf16[512,128]{1,0:T(8,128)(2,1)S(1)}, bf16[512,128]{1,0:T(8,128)(2,1)S(1)}, u32[]{:S(2)}, u32[]{:S(2)}) %collective-permute-start.1) | collective-permute-done | bytes 131104 | tf_op jit(solution)/shard_map/ppermute | solution.py:439
  52.0 0.0 copy-start.2
  52.0 1.9 %collective-permute-start.3 = (bf16[512,128]{1,0:T(8,128)(2,1)S(1)}, bf16[512,128]{1,0:T(8,128)(2,1)S(1)}, u32[]{:S(2)}, u32[]{:S(2)}) collective-permute-start(bf16[512,128]{1,0:T(8,128)(2,1)S(1)} %collective-permute-done.1.refs_2_), channel_id=1, source_target_pairs={{7,0},{0,1},{1,2},{2,3},{3,4},{4,5},{5,6},{6,7},{15,8},{8,9},{9,10... | collective-permute-start | bytes 393224 | tf_op jit(solution)/shard_map/ppermute | solution.py:439
  54.0 0.0 collective-permute-done.refs_1_
  54.0 0.0 copy-start.3
  54.0 5.1 %collective-permute-start.2 = (bf16[512,128]{1,0:T(8,128)(2,1)S(1)}, bf16[512,128]{1,0:T(8,128)(2,1)S(1)}, u32[]{:S(2)}, u32[]{:S(2)}) collective-permute-start(bf16[512,128]{1,0:T(8,128)(2,1)S(1)} %collective-permute-done.refs_1_), channel_id=1, source_target_pairs={{1,0},{2,1},{3,2},{4,3},{5,4},{6,5},{7,6},{0,7},{9,8},{10,9},{11,1... | collective-permute-start | bytes 393224 | tf_op jit(solution)/shard_map/ppermute | solution.py:439
  59.1 4.8 %collective-permute-start.6 = (bf16[512,128]{1,0:T(8,128)(2,1)S(1)}, bf16[512,128]{1,0:T(8,128)(2,1)S(1)}, u32[]{:S(2)}, u32[]{:S(2)}) collective-permute-start(bf16[512,128]{1,0:T(8,128)(2,1)S(1)} %pad_maximum_fusion.refs_0_), channel_id=1, source_target_pairs={{4,0},{5,1},{6,2},{7,3},{0,4},{1,5},{2,6},{3,7},{12,8},{13,9},{14,... | collective-permute-start | bytes 393224 | tf_op jit(solution)/shard_map/ppermute | solution.py:439
  64.0 0.0 collective-permute-done.3.refs_4_
  64.0 0.0 copy-start.4
  64.0 1.9 %collective-permute-start.5 = (bf16[512,128]{1,0:T(8,128)(2,1)S(1)}, bf16[512,128]{1,0:T(8,128)(2,1)S(1)}, u32[]{:S(2)}, u32[]{:S(2)}) collective-permute-start(bf16[512,128]{1,0:T(8,128)(2,1)S(1)} %collective-permute-done.3.refs_4_), channel_id=1, source_target_pairs={{7,0},{0,1},{1,2},{2,3},{3,4},{4,5},{5,6},{6,7},{15,8},{8,9},{9,10... | collective-permute-start | bytes 393224 | tf_op jit(solution)/shard_map/ppermute | solution.py:439
  65.9 0.0 collective-permute-done.2.refs_3_
  65.9 0.0 copy-start.5
  65.9 5.1 %collective-permute-start.4 = (bf16[512,128]{1,0:T(8,128)(2,1)S(1)}, bf16[512,128]{1,0:T(8,128)(2,1)S(1)}, u32[]{:S(2)}, u32[]{:S(2)}) collective-permute-start(bf16[512,128]{1,0:T(8,128)(2,1)S(1)} %collective-permute-done.2.refs_3_), channel_id=1, source_target_pairs={{1,0},{2,1},{3,2},{4,3},{5,4},{6,5},{7,6},{0,7},{9,8},{10,9},{11,1... | collective-permute-start | bytes 393224 | tf_op jit(solution)/shard_map/ppermute | solution.py:439
  71.1 0.1 pad_add_fusion.place
  71.1 1.5 %collective-permute-done.6.refs_7_ = bf16[512,128]{1,0:T(8,128)(2,1)S(1)} collective-permute-done((bf16[512,128]{1,0:T(8,128)(2,1)S(1)}, bf16[512,128]{1,0:T(8,128)(2,1)S(1)}, u32[]{:S(2)}, u32[]{:S(2)}) %collective-permute-start.6) | collective-permute-done | bytes 131104 | tf_op jit(solution)/shard_map/ppermute | solution.py:439
  72.7 0.0 copy-start.6
  72.7 1.1 collective-permute-done.5.refs_6_
  73.8 0.0 copy-start.7
  73.8 0.0 collective-permute-done.4.refs_5_
  73.8 0.0 copy-start.8
  73.8 0.0 collective-permute-done.7.refs_9_
  73.8 0.0 copy-done
  73.8 0.0 copy-done.1
  73.8 0.0 copy-done.2
  73.8 0.0 copy-done.3
  73.8 0.0 copy-done.4
  73.8 0.0 copy-done.5
  73.8 0.0 copy-done.6
  73.9 0.6 copy-done.7
  74.4 0.1 copy-done.8
  74.5 22.1 %shard_map.75 = (bf16[256,128]{1,0:T(8,128)(2,1)}, f32[256,128]{1,0:T(8,128)S(1)}, bf16[2048,128]{1,0:T(8,128)(2,1)S(1)}, bf16[8,8,16,128]{3,2,1,0:T(8,128)(2,1)S(1)}, bf16[384,1152]{1,0:T(8,128)(2,1)S(1)}) custom-call(s32[2]{0:T(128)S(1)} %pad_add_fusion.place, bf16[512,128]{1,0:T(8,128)(2,1)} %copy-done.1, bf16[512,128]{1,0:T(8,128)(2,1)} %copy-done.3, ...), custom_call_target="tpu_custom_call" | custom-call | tf_op jit(solution)/shard_map/pallas_call | solution.py:338
  96.5 9.9 %all_to_all.22.parts = bf16[8,8,16,128]{3,2,1,0:T(8,128)(2,1)S(1)} all-to-all(bf16[8,8,16,128]{3,2,1,0:T(8,128)(2,1)S(1)} %get-tuple-element.15), channel_id=1, replica_groups=mesh['y'=8,'x'=4,'core'=2,'space'=8] {'x','core'}, dimensions={0} | all-to-all | bytes 524288 | tf_op jit(solution)/shard_map/all_to_all | solution.py:471
  106.5 0.7 broadcast_in_dim.8
  107.2 7.1 %all-to-all-start.3 = ((bf16[64,16,128]{2,1,0:T(8,128)(2,1)}), bf16[64,16,128]{2,1,0:T(8,128)(2,1)S(1)}, u32[]{:S(2)}, u32[]{:S(2)}) async-start(bf16[64,16,128]{2,1,0:T(8,128)(2,1)} %bitcast.6), calls=%async_computation.3 | async-start | bytes 524288 | tf_op jit(solution)/shard_map/all_to_all | solution.py:475
  114.3 2.1 %shard_map.76 = bf16[256,128]{1,0:T(8,128)(2,1)} custom-call(s32[2]{0:T(128)S(1)} %pad_add_fusion.place, bf16[2048,128]{1,0:T(8,128)(2,1)S(1)} %get-tuple-element.12.delta, bf16[384,1152]{1,0:T(8,128)(2,1)S(1)} %get-tuple-element.13.weight, f32[256,128]{1,0:T(8,128)S(1)} %get-tuple-element.14.outer_slab), custom_call_target="tpu_custom_call" | custom-call | tf_op jit(solution)/shard_map/pallas_call | solution.py:338
  116.5 12.5 %all-to-all-done.3 = bf16[64,16,128]{2,1,0:T(8,128)(2,1)S(1)} async-done(((bf16[64,16,128]{2,1,0:T(8,128)(2,1)}), bf16[64,16,128]{2,1,0:T(8,128)(2,1)S(1)}, u32[]{:S(2)}, u32[]{:S(2)}) %all-to-all-start.3) | async-done | bytes 262176 | tf_op jit(solution)/shard_map/all_to_all | solution.py:475
  128.9 0.7 shard_map.78
  (3 shorter events, 0.1 us)
Async XLA Ops:
  19.6 17.3 %copy-start.9 = (bf16[1,4,8,8,128]{4,3,2,1,0:T(8,128)(2,1)S(1)}, bf16[1,4,8,8,128]{4,3,2,1,0:T(8,128)(2,1)}, u32[]{:S(2)}) copy-start(bf16[1,4,8,8,128]{4,3,2,1,0:T(8,128)(2,1)} %param.5) | copy-start | bytes 196612
  19.6 17.3 %copy-start.10 = (bf16[1,4,8,8,128]{4,3,2,1,0:T(8,128)(2,1)S(1)}, bf16[1,4,8,8,128]{4,3,2,1,0:T(8,128)(2,1)}, u32[]{:S(2)}) copy-start(bf16[1,4,8,8,128]{4,3,2,1,0:T(8,128)(2,1)} %param.4) | copy-start | bytes 196612
  35.0 38.8 %copy-start = (bf16[4,8,112,128]{3,2,1,0:T(8,128)(2,1)}, bf16[4,8,112,128]{3,2,1,0:T(8,128)(2,1)S(1)}, u32[]{:S(2)}) copy-start(bf16[4,8,112,128]{3,2,1,0:T(8,128)(2,1)S(1)} %all_to_all.21.refs_8_) | copy-start | bytes 2752516
  35.0 38.8 %collective-permute-start.7 = (bf16[4,8,112,128]{3,2,1,0:T(8,128)(2,1)S(1)}, bf16[4,8,112,128]{3,2,1,0:T(8,128)(2,1)}, u32[]{:S(2)}, u32[]{:S(2)}) collective-permute-start(bf16[4,8,112,128]{3,2,1,0:T(8,128)(2,1)S(1)} %all_to_all.21.refs_8_), channel_id=1, source_target_pairs={{0,8},{8,0},{1,9},{9,1},{2,10},{10,2},{3,11},{11,3},{4,12},{12,4},... | collective-permute-start | bytes 2752520 | tf_op jit(solution)/shard_map/ppermute | solution.py:467
  36.9 36.9 %copy-start.1 = (bf16[512,128]{1,0:T(8,128)(2,1)}, bf16[512,128]{1,0:T(8,128)(2,1)S(1)}, u32[]{:S(2)}) copy-start(bf16[512,128]{1,0:T(8,128)(2,1)S(1)} %pad_maximum_fusion.refs_0_) | copy-start | bytes 393220
  36.9 15.1 %collective-permute-start.1 = (bf16[512,128]{1,0:T(8,128)(2,1)S(1)}, bf16[512,128]{1,0:T(8,128)(2,1)S(1)}, u32[]{:S(2)}, u32[]{:S(2)}) collective-permute-start(bf16[512,128]{1,0:T(8,128)(2,1)S(1)} %pad_maximum_fusion.refs_0_), channel_id=1, source_target_pairs={{7,0},{0,1},{1,2},{2,3},{3,4},{4,5},{5,6},{6,7},{15,8},{8,9},{9,10... | collective-permute-start | bytes 393224 | tf_op jit(solution)/shard_map/ppermute | solution.py:439
  41.2 12.7 %collective-permute-start = (bf16[512,128]{1,0:T(8,128)(2,1)S(1)}, bf16[512,128]{1,0:T(8,128)(2,1)S(1)}, u32[]{:S(2)}, u32[]{:S(2)}) collective-permute-start(bf16[512,128]{1,0:T(8,128)(2,1)S(1)} %pad_maximum_fusion.refs_0_), channel_id=1, source_target_pairs={{1,0},{2,1},{3,2},{4,3},{5,4},{6,5},{7,6},{0,7},{9,8},{10,9},{11,1... | collective-permute-start | bytes 393224 | tf_op jit(solution)/shard_map/ppermute | solution.py:439
  52.0 21.8 %copy-start.2 = (bf16[512,128]{1,0:T(8,128)(2,1)}, bf16[512,128]{1,0:T(8,128)(2,1)S(1)}, u32[]{:S(2)}) copy-start(bf16[512,128]{1,0:T(8,128)(2,1)S(1)} %collective-permute-done.1.refs_2_) | copy-start | bytes 393220
  52.0 11.9 %collective-permute-start.3 = (bf16[512,128]{1,0:T(8,128)(2,1)S(1)}, bf16[512,128]{1,0:T(8,128)(2,1)S(1)}, u32[]{:S(2)}, u32[]{:S(2)}) collective-permute-start(bf16[512,128]{1,0:T(8,128)(2,1)S(1)} %collective-permute-done.1.refs_2_), channel_id=1, source_target_pairs={{7,0},{0,1},{1,2},{2,3},{3,4},{4,5},{5,6},{6,7},{15,8},{8,9},{9,10... | collective-permute-start | bytes 393224 | tf_op jit(solution)/shard_map/ppermute | solution.py:439
  54.0 19.8 %copy-start.3 = (bf16[512,128]{1,0:T(8,128)(2,1)}, bf16[512,128]{1,0:T(8,128)(2,1)S(1)}, u32[]{:S(2)}) copy-start(bf16[512,128]{1,0:T(8,128)(2,1)S(1)} %collective-permute-done.refs_1_) | copy-start | bytes 393220
  54.0 11.9 %collective-permute-start.2 = (bf16[512,128]{1,0:T(8,128)(2,1)S(1)}, bf16[512,128]{1,0:T(8,128)(2,1)S(1)}, u32[]{:S(2)}, u32[]{:S(2)}) collective-permute-start(bf16[512,128]{1,0:T(8,128)(2,1)S(1)} %collective-permute-done.refs_1_), channel_id=1, source_target_pairs={{1,0},{2,1},{3,2},{4,3},{5,4},{6,5},{7,6},{0,7},{9,8},{10,9},{11,1... | collective-permute-start | bytes 393224 | tf_op jit(solution)/shard_map/ppermute | solution.py:439
  59.1 13.6 %collective-permute-start.6 = (bf16[512,128]{1,0:T(8,128)(2,1)S(1)}, bf16[512,128]{1,0:T(8,128)(2,1)S(1)}, u32[]{:S(2)}, u32[]{:S(2)}) collective-permute-start(bf16[512,128]{1,0:T(8,128)(2,1)S(1)} %pad_maximum_fusion.refs_0_), channel_id=1, source_target_pairs={{4,0},{5,1},{6,2},{7,3},{0,4},{1,5},{2,6},{3,7},{12,8},{13,9},{14,... | collective-permute-start | bytes 393224 | tf_op jit(solution)/shard_map/ppermute | solution.py:439
  64.0 9.9 %copy-start.4 = (bf16[512,128]{1,0:T(8,128)(2,1)}, bf16[512,128]{1,0:T(8,128)(2,1)S(1)}, u32[]{:S(2)}) copy-start(bf16[512,128]{1,0:T(8,128)(2,1)S(1)} %collective-permute-done.3.refs_4_) | copy-start | bytes 393220
  64.0 9.8 %collective-permute-start.5 = (bf16[512,128]{1,0:T(8,128)(2,1)S(1)}, bf16[512,128]{1,0:T(8,128)(2,1)S(1)}, u32[]{:S(2)}, u32[]{:S(2)}) collective-permute-start(bf16[512,128]{1,0:T(8,128)(2,1)S(1)} %collective-permute-done.3.refs_4_), channel_id=1, source_target_pairs={{7,0},{0,1},{1,2},{2,3},{3,4},{4,5},{5,6},{6,7},{15,8},{8,9},{9,10... | collective-permute-start | bytes 393224 | tf_op jit(solution)/shard_map/ppermute | solution.py:439
  65.9 7.9 %copy-start.5 = (bf16[512,128]{1,0:T(8,128)(2,1)}, bf16[512,128]{1,0:T(8,128)(2,1)S(1)}, u32[]{:S(2)}) copy-start(bf16[512,128]{1,0:T(8,128)(2,1)S(1)} %collective-permute-done.2.refs_3_) | copy-start | bytes 393220
  65.9 7.9 %collective-permute-start.4 = (bf16[512,128]{1,0:T(8,128)(2,1)S(1)}, bf16[512,128]{1,0:T(8,128)(2,1)S(1)}, u32[]{:S(2)}, u32[]{:S(2)}) collective-permute-start(bf16[512,128]{1,0:T(8,128)(2,1)S(1)} %collective-permute-done.2.refs_3_), channel_id=1, source_target_pairs={{1,0},{2,1},{3,2},{4,3},{5,4},{6,5},{7,6},{0,7},{9,8},{10,9},{11,1... | collective-permute-start | bytes 393224 | tf_op jit(solution)/shard_map/ppermute | solution.py:439
  72.7 1.2 copy-start.6
  73.8 0.7 copy-start.7
  73.8 0.7 copy-start.8
  107.2 21.7 %all-to-all-start.3 = ((bf16[64,16,128]{2,1,0:T(8,128)(2,1)}), bf16[64,16,128]{2,1,0:T(8,128)(2,1)S(1)}, u32[]{:S(2)}, u32[]{:S(2)}) async-start(bf16[64,16,128]{2,1,0:T(8,128)(2,1)} %bitcast.6), calls=%async_computation.3 | async-start | bytes 524288 | tf_op jit(solution)/shard_map/all_to_all | solution.py:475

commit v2 on v1

--- a/solution.py
+++ b/solution.py
@@ -59,9 +59,8 @@
         out[pl.ds(row, rows), b * C : (b + 1) * C] = y.reshape(rows, C).astype(bf16)
 
 
-def conv_into(acc, source, weight, planes, step, turned=None):
+def conv_into(acc, source, weight, planes, step, turned=None, prepare=None, beside=None):
     rows = step * PLANE
-
     margin = 2 * PLANE
 
     def clear(i, _):
@@ -70,27 +69,27 @@
         return 0
 
     lax.fori_loop(0, (planes + 2) // 2, clear, 0)
-
-    def one(i, _):
-        row = pl.multiple_of(i * rows, rows)
-        z = jnp.dot(source[pl.ds(row, rows), :], weight[...], preferred_element_type=f32)
+    prepare = prepare or (lambda row: None)
+    prepare(0)
+    for row in range(0, planes * PLANE, rows):
+        if row + rows < planes * PLANE:
+            prepare(row + rows)
+        elif beside is not None:
+            beside()
+        z = jnp.dot(source[row : row + rows, :], weight[...], preferred_element_type=f32)
         for a in range(3):
             x = [
                 z[:, (3 * a + b) * C : (3 * a + b + 1) * C].reshape(step, H, W, C)
                 for b in range(3)
             ]
             total = h_down(x[0]) + x[1] + h_up(x[2])
-            at = pl.ds(pl.multiple_of(row + (2 - a) * PLANE, PLANE), rows)
-            acc[at, :] += total.reshape(rows, C)
+            top = row + (2 - a) * PLANE
+            acc[top : top + rows, :] += total.reshape(rows, C)
         if turned is not None:
-            for n in range(rows // C):
-                at = pl.multiple_of(row + n * C, C)
+            for at in range(row, row + rows, C):
                 for c in range(3):
-                    block = source[pl.ds(at, C), c * C : (c + 1) * C]
-                    turned[c * C : (c + 1) * C, pl.ds(at, C)] = block.T
-        return 0
-
-    lax.fori_loop(0, planes // step, one, 0)
+                    block = source[at : at + C, c * C : (c + 1) * C]
+                    turned[c * C : (c + 1) * C, at : at + C] = block.T
 
 
 def by_taps(flat, weight):
@@ -109,12 +108,12 @@
 
 
 def assemble(core, mine, theirs, flat, weight):
-    across, chips = mine.shape[0], mine.shape[0] * mine.shape[1]
+    chips = mine.shape[0]
     part = ROWS // (2 * chips)
     mine_first = core == 0
     for y in range(chips):
-        one = mine[y % across, y // across].astype(f32)
-        two = theirs[y % across, y // across].astype(f32)
+        one = mine[y].astype(f32)
+        two = theirs[y].astype(f32)
         even = jnp.where(mine_first, one, two)[:part]
         odd = jnp.where(mine_first, two, one)[:part]
         flat[2 * y * part : (2 * y + 1) * part, :] = even
@@ -177,14 +176,14 @@
         output, outer_out, delta_out, grads_out, weight_out,
         image, cotangent, first_delta, outer_slab, grads,
         mine1, theirs1, mine2, theirs2, weight1, weight2, turned_weight,
-        image_three, three, delta_three, image_turned, turned, normed, conv, outer, flat,
+        image_three, three, delta_three, image_turned, turned, normed, conv, conv2, outer, flat,
         image_sem, other_sem, weight_sem, out_sem,
     ) = refs
     cells = image.shape[0]
     planes = cells // PLANE
     slab = output.shape[0]
     count = cells // slab
-    padded = mine1.shape[2]
+    padded = mine1.shape[1]
     zero = jnp.zeros((1, C), f32)
     copy = pltpu.make_async_copy
     fields = ([], [])
@@ -197,7 +196,7 @@
             copy(block.at[row + slab : row + 2 * slab], cotangent.at[at], other_sem.at[n])
         )
     weights = [
-        copy(source.at[:, :, half * padded : (half + 1) * padded], target, weight_sem.at[n])
+        copy(source.at[:, half * padded : (half + 1) * padded], target, weight_sem.at[n])
         for n, (source, half, target) in enumerate(
             ((mine, 0, mine1), (theirs, 0, theirs1), (mine, 1, mine2), (theirs, 1, theirs2))
         )
@@ -210,39 +209,44 @@
     for c in fields[0]:
         c.wait()
 
-    def shift_image(i, row, _):
-        put_w_shifts(image[pl.ds(row, BLOCK), :].astype(f32), image_three, row)
-        return 0
-
-    blocks_of(cells, shift_image, 0)
-    for c in weights[:2]:
+    def each(row, body):
+        for n in range(row, row + STEP * PLANE, BLOCK):
+            body(n)
+
+    def shift_image(n):
+        put_w_shifts(image[n : n + BLOCK, :].astype(f32), image_three, n)
+
+    for c in weights:
         c.wait()
     assemble(place[1], mine1, theirs1, flat, weight1)
     weight_copy = copy(weight1, weight_out, out_sem.at[0])
     weight_copy.start()
-    conv_into(conv, image_three, weight1, planes, STEP, image_turned)
+    conv_into(
+        conv, image_three, weight1, planes, STEP, image_turned,
+        lambda row: each(row, shift_image),
+        lambda: assemble(place[1], mine2, theirs2, flat, weight2),
+    )
     average1, inverse1 = statistics(conv, cells)
 
-    def norm_one(i, row, _):
-        u = (conv[pl.ds(row + PLANE, BLOCK), :] - average1) * inverse1
-        normed[pl.ds(row, BLOCK), :] = u
-        put_w_shifts(u * phi_parts(u), three, row)
-        return 0
-
-    blocks_of(cells, norm_one, 0)
-    for c in weights[2:]:
-        c.wait()
-    assemble(place[1], mine2, theirs2, flat, weight2)
-    conv_into(conv, three, weight2, planes, STEP, turned)
-    average, inverse = statistics(conv, cells)
+    def norm_one(n):
+        u = (conv[n + PLANE : n + PLANE + BLOCK, :] - average1) * inverse1
+        normed[n : n + BLOCK, :] = u
+        put_w_shifts(u * phi_parts(u), three, n)
+
+    conv_into(
+        conv2, three, weight2, planes, STEP, turned,
+        lambda row: each(row, norm_one),
+        lambda: reverse_into(weight2, turned_weight),
+    )
+    average, inverse = statistics(conv2, cells)
     for c in fields[1]:
         c.wait()
     parts = slab // BLOCK
 
     def norm_two(i, row, sums):
         at = pl.ds(row, BLOCK)
-        n = (conv[pl.ds(row + PLANE, BLOCK), :] - average) * inverse
-        conv[pl.ds(row + PLANE, BLOCK), :] = n
+        n = (conv2[pl.ds(row + PLANE, BLOCK), :] - average) * inverse
+        conv2[pl.ds(row + PLANE, BLOCK), :] = n
         u = image[at, :].astype(f32) + n
         cdf = phi_parts(u)
         grad = cotangent[at, :].astype(f32) * slope_of(u, cdf)
@@ -263,7 +267,7 @@
     paired = paired / cells
 
     def back_two(i, row, _):
-        n = conv[pl.ds(row + PLANE, BLOCK), :]
+        n = conv2[pl.ds(row + PLANE, BLOCK), :]
         value = inverse * (outer[pl.ds(row, BLOCK), :] - plain - n * paired)
         put_w_shifts(value, three, row)
         put_h_shifts(value, delta_three, row + PLANE)
@@ -273,7 +277,6 @@
     half = grads.shape[2] // 2
     grad_into(turned, delta_three, cells, flat, grads, place, half)
 
-    reverse_into(weight2, turned_weight)
     conv_into(conv, three, turned_weight, planes, STEP)
 
     def inner_grad(i, row, sums):
@@ -351,7 +354,7 @@
     offsets = [(o, n) for many, _ in blocks for n, o in enumerate(many)]
     arrays = [array for many, array in blocks for _ in many]
     field = (cells, C)
-    half = mine.shape[:2] + (mine.shape[2] // 2, C)
+    half = (mine.shape[0], mine.shape[1] // 2, C)
     local = pltpu.VMEM
     signal = pltpu.SemaphoreType.DMA
     return call(
@@ -368,7 +371,8 @@
             local((cells, 3 * C), bf16), local((cells, 3 * C), bf16),
             local((cells + 2 * PLANE, 3 * C), bf16),
             local((3 * C, cells), bf16), local((3 * C, cells), bf16),
-            local(field, f32), local((cells + 2 * PLANE, C), f32), local(field, f32),
+            local(field, f32), local((cells + 2 * PLANE, C), f32),
+            local((cells + 2 * PLANE, C), f32), local(field, f32),
             local((ROWS + 8, C), f32),
             signal((count,)), signal((count,)), signal((4,)), signal((4,)),
         ],
@@ -460,8 +464,7 @@
 
         tall = ((0, padded - part), (0, 0))
         shard = jnp.concatenate([jnp.pad(first_weight, tall), jnp.pad(second_weight, tall)])
-        column = spread(shard, "y", far)
-        mine = spread(column, "x", across)
+        mine = spread(shard, ("y", "x"), far * across)
         pair = jnp.concatenate([image.reshape(slab, C), cotangent.reshape(slab, C)])
         blocks = whole_patch(pair)
         theirs = lax.ppermute(mine, "core", swap)

time: 130 us -> 133 us (1.023)
  blocking collectives: 43.3 us -> 46.1 us
    all_to_all x2 -> x1, blocking collectives: 33.4 us -> 35.4 us  [spread(): return lax.all_to_all(copies, axes, 0, 0, tiled=True)]
where the time goes in v2:
time: 133 us; the launch traced here: 132 us
  blocking collectives  46.1 us (35%)
  starting transfers between devices  40.3 us (30%)
  Pallas kernels  25.1 us (19%)
  waiting for transfers between devices  17.3 us (13%)
  local copies, waits for them, and re-layouts  1.52 us (1%)
    all_to_all x1, blocking collectives, spread(): return lax.all_to_all(copies, axes, 0, 0, tiled=True)  35.4 us
    ppermute x7, starting transfers between devices, shifted(): return lax.ppermute(x, 'space', pairs)  31.8 us
    pallas_call x4, Pallas kernels, call(): pl.pallas_call(kernel, out_shape=tuple((jax.ShapeDtypeStruct(s, d) for s,...  25.1 us
    all_to_all x1, waiting for transfers between devices, step(): lax.all_to_all(spaced.reshape((far * space,) + sums.shape[1:]), ('y', 'sp...  12.5 us
    all_to_all x1, blocking collectives, step(): parts = lax.all_to_all(grads, ('x', 'core'), 0, 0, tiled=True)  10.7 us
    all_to_all x1, starting transfers between devices, step(): lax.all_to_all(spaced.reshape((far * space,) + sums.shape[1:]), ('y', 'sp...  6.63 us
    ppermute x7, waiting for transfers between devices, shifted(): return lax.ppermute(x, 'space', pairs)  4.85 us
  transfers between devices with their start and end apart: 9, of which 4 were waited for; matrix products, arithmetic and copies ran while one was open for 0% of the time, Pallas kernels for 2%

profile of v2, /device:TPU:2, one launch (start us, length us, event | category | flops | bytes accessed | tf_op | source)
XLA Modules:
  0.0 132.1 jit_solution(16665061103244699018)
XLA Ops:
  0.6 0.7 fusion.2
  1.4 0.1 broadcast_in_dim.4
  1.5 0.0 copy-start.9
  1.5 0.0 copy-start.10
  1.5 35.4 %all_to_all.15.refs_8_ = bf16[32,112,128]{2,1,0:T(8,128)(2,1)S(1)} all-to-all(bf16[32,112,128]{2,1,0:T(8,128)(2,1)S(1)} %broadcast_in_dim.4), channel_id=1, replica_groups=mesh['y'=8,'x'=4,'core'=2,'space'=8] {'y','x'}, dimensions={0} | all-to-all | bytes 1835008 | tf_op jit(solution)/shard_map/all_to_all | solution.py:427
  37.0 0.0 copy-start
  37.0 1.9 %collective-permute-start.7 = (bf16[32,112,128]{2,1,0:T(8,128)(2,1)S(1)}, bf16[32,112,128]{2,1,0:T(8,128)(2,1)}, u32[]{:S(2)}, u32[]{:S(2)}) collective-permute-start(bf16[32,112,128]{2,1,0:T(8,128)(2,1)S(1)} %all_to_all.15.refs_8_), channel_id=1, source_target_pairs={{0,8},{8,0},{1,9},{9,1},{2,10},{10,2},{3,11},{11,3},{4,12},{12,4},... | collective-permute-start | bytes 2752520 | tf_op jit(solution)/shard_map/ppermute | solution.py:470
  38.9 0.0 copy-done.9
  38.9 0.0 copy-done.10
  38.9 0.0 copy-start.1
  38.9 4.3 %collective-permute-start.1 = (bf16[512,128]{1,0:T(8,128)(2,1)S(1)}, bf16[512,128]{1,0:T(8,128)(2,1)S(1)}, u32[]{:S(2)}, u32[]{:S(2)}) collective-permute-start(bf16[512,128]{1,0:T(8,128)(2,1)S(1)} %pad_maximum_fusion.refs_0_), channel_id=1, source_target_pairs={{7,0},{0,1},{1,2},{2,3},{3,4},{4,5},{5,6},{6,7},{15,8},{8,9},{9,10... | collective-permute-start | bytes 393224 | tf_op jit(solution)/shard_map/ppermute | solution.py:443
  43.2 8.6 %collective-permute-start = (bf16[512,128]{1,0:T(8,128)(2,1)S(1)}, bf16[512,128]{1,0:T(8,128)(2,1)S(1)}, u32[]{:S(2)}, u32[]{:S(2)}) collective-permute-start(bf16[512,128]{1,0:T(8,128)(2,1)S(1)} %pad_maximum_fusion.refs_0_), channel_id=1, source_target_pairs={{1,0},{2,1},{3,2},{4,3},{5,4},{6,5},{7,6},{0,7},{9,8},{10,9},{11,1... | collective-permute-start | bytes 393224 | tf_op jit(solution)/shard_map/ppermute | solution.py:443
  51.8 2.2 %collective-permute-done.1.refs_2_ = bf16[512,128]{1,0:T(8,128)(2,1)S(1)} collective-permute-done((bf16[512,128]{1,0:T(8,128)(2,1)S(1)}, bf16[512,128]{1,0:T(8,128)(2,1)S(1)}, u32[]{:S(2)}, u32[]{:S(2)}) %collective-permute-start.1) | collective-permute-done | bytes 131104 | tf_op jit(solution)/shard_map/ppermute | solution.py:443
  54.0 0.0 copy-start.2
  54.0 1.9 %collective-permute-start.3 = (bf16[512,128]{1,0:T(8,128)(2,1)S(1)}, bf16[512,128]{1,0:T(8,128)(2,1)S(1)}, u32[]{:S(2)}, u32[]{:S(2)}) collective-permute-start(bf16[512,128]{1,0:T(8,128)(2,1)S(1)} %collective-permute-done.1.refs_2_), channel_id=1, source_target_pairs={{7,0},{0,1},{1,2},{2,3},{3,4},{4,5},{5,6},{6,7},{15,8},{8,9},{9,10... | collective-permute-start | bytes 393224 | tf_op jit(solution)/shard_map/ppermute | solution.py:443
  55.9 0.0 collective-permute-done.refs_1_
  56.0 0.0 copy-start.3
  56.0 5.1 %collective-permute-start.2 = (bf16[512,128]{1,0:T(8,128)(2,1)S(1)}, bf16[512,128]{1,0:T(8,128)(2,1)S(1)}, u32[]{:S(2)}, u32[]{:S(2)}) collective-permute-start(bf16[512,128]{1,0:T(8,128)(2,1)S(1)} %collective-permute-done.refs_1_), channel_id=1, source_target_pairs={{1,0},{2,1},{3,2},{4,3},{5,4},{6,5},{7,6},{0,7},{9,8},{10,9},{11,1... | collective-permute-start | bytes 393224 | tf_op jit(solution)/shard_map/ppermute | solution.py:443
  61.1 4.8 %collective-permute-start.6 = (bf16[512,128]{1,0:T(8,128)(2,1)S(1)}, bf16[512,128]{1,0:T(8,128)(2,1)S(1)}, u32[]{:S(2)}, u32[]{:S(2)}) collective-permute-start(bf16[512,128]{1,0:T(8,128)(2,1)S(1)} %pad_maximum_fusion.refs_0_), channel_id=1, source_target_pairs={{4,0},{5,1},{6,2},{7,3},{0,4},{1,5},{2,6},{3,7},{12,8},{13,9},{14,... | collective-permute-start | bytes 393224 | tf_op jit(solution)/shard_map/ppermute | solution.py:443
  65.9 0.0 collective-permute-done.3.refs_4_
  65.9 0.0 copy-start.4
  66.0 1.9 %collective-permute-start.5 = (bf16[512,128]{1,0:T(8,128)(2,1)S(1)}, bf16[512,128]{1,0:T(8,128)(2,1)S(1)}, u32[]{:S(2)}, u32[]{:S(2)}) collective-permute-start(bf16[512,128]{1,0:T(8,128)(2,1)S(1)} %collective-permute-done.3.refs_4_), channel_id=1, source_target_pairs={{7,0},{0,1},{1,2},{2,3},{3,4},{4,5},{5,6},{6,7},{15,8},{8,9},{9,10... | collective-permute-start | bytes 393224 | tf_op jit(solution)/shard_map/ppermute | solution.py:443
  67.9 0.0 collective-permute-done.2.refs_3_
  67.9 0.0 copy-start.5
  67.9 5.1 %collective-permute-start.4 = (bf16[512,128]{1,0:T(8,128)(2,1)S(1)}, bf16[512,128]{1,0:T(8,128)(2,1)S(1)}, u32[]{:S(2)}, u32[]{:S(2)}) collective-permute-start(bf16[512,128]{1,0:T(8,128)(2,1)S(1)} %collective-permute-done.2.refs_3_), channel_id=1, source_target_pairs={{1,0},{2,1},{3,2},{4,3},{5,4},{6,5},{7,6},{0,7},{9,8},{10,9},{11,1... | collective-permute-start | bytes 393224 | tf_op jit(solution)/shard_map/ppermute | solution.py:443
  73.0 0.1 pad_add_fusion.place
  73.1 1.5 %collective-permute-done.6.refs_7_ = bf16[512,128]{1,0:T(8,128)(2,1)S(1)} collective-permute-done((bf16[512,128]{1,0:T(8,128)(2,1)S(1)}, bf16[512,128]{1,0:T(8,128)(2,1)S(1)}, u32[]{:S(2)}, u32[]{:S(2)}) %collective-permute-start.6) | collective-permute-done | bytes 131104 | tf_op jit(solution)/shard_map/ppermute | solution.py:443
  74.7 0.0 copy-start.6
  74.7 1.1 collective-permute-done.5.refs_6_
  75.7 0.0 copy-start.7
  75.7 0.0 collective-permute-done.4.refs_5_
  75.8 0.0 copy-start.8
  75.8 0.0 collective-permute-done.7.refs_9_
  75.8 0.0 copy-done
  75.8 0.0 copy-done.1
  75.8 0.0 copy-done.2
  75.8 0.0 copy-done.3
  75.8 0.0 copy-done.4
  75.8 0.0 copy-done.5
  75.8 0.0 copy-done.6
  75.8 0.6 copy-done.7
  76.4 0.1 copy-done.8
  76.5 22.3 %shard_map.75 = (bf16[256,128]{1,0:T(8,128)(2,1)}, f32[256,128]{1,0:T(8,128)S(1)}, bf16[2048,128]{1,0:T(8,128)(2,1)S(1)}, bf16[8,8,16,128]{3,2,1,0:T(8,128)(2,1)S(1)}, bf16[384,1152]{1,0:T(8,128)(2,1)S(1)}) custom-call(s32[2]{0:T(128)S(1)} %pad_add_fusion.place, bf16[512,128]{1,0:T(8,128)(2,1)} %copy-done.1, bf16[512,128]{1,0:T(8,128)(2,1)} %copy-done.3, ...), custom_call_target="tpu_custom_call" | custom-call | tf_op jit(solution)/shard_map/pallas_call | solution.py:341
  98.8 10.7 %all_to_all.16.parts = bf16[8,8,16,128]{3,2,1,0:T(8,128)(2,1)S(1)} all-to-all(bf16[8,8,16,128]{3,2,1,0:T(8,128)(2,1)S(1)} %get-tuple-element.15), channel_id=1, replica_groups=mesh['y'=8,'x'=4,'core'=2,'space'=8] {'x','core'}, dimensions={0} | all-to-all | bytes 524288 | tf_op jit(solution)/shard_map/all_to_all | solution.py:474
  109.4 0.7 broadcast_in_dim.5
  110.2 6.6 %all-to-all-start.2 = ((bf16[64,16,128]{2,1,0:T(8,128)(2,1)}), bf16[64,16,128]{2,1,0:T(8,128)(2,1)S(1)}, u32[]{:S(2)}, u32[]{:S(2)}) async-start(bf16[64,16,128]{2,1,0:T(8,128)(2,1)} %bitcast.6), calls=%async_computation.2 | async-start | bytes 524288 | tf_op jit(solution)/shard_map/all_to_all | solution.py:478
  116.8 2.1 %shard_map.76 = bf16[256,128]{1,0:T(8,128)(2,1)} custom-call(s32[2]{0:T(128)S(1)} %pad_add_fusion.place, bf16[2048,128]{1,0:T(8,128)(2,1)S(1)} %get-tuple-element.12.delta, bf16[384,1152]{1,0:T(8,128)(2,1)S(1)} %get-tuple-element.13.weight, f32[256,128]{1,0:T(8,128)S(1)} %get-tuple-element.14.outer_slab), custom_call_target="tpu_custom_call" | custom-call | tf_op jit(solution)/shard_map/pallas_call | solution.py:341
  118.9 12.5 %all-to-all-done.2 = bf16[64,16,128]{2,1,0:T(8,128)(2,1)S(1)} async-done(((bf16[64,16,128]{2,1,0:T(8,128)(2,1)}), bf16[64,16,128]{2,1,0:T(8,128)(2,1)S(1)}, u32[]{:S(2)}, u32[]{:S(2)}) %all-to-all-start.2) | async-done | bytes 262176 | tf_op jit(solution)/shard_map/all_to_all | solution.py:478
  131.4 0.7 shard_map.78
  (2 shorter events, 0.1 us)
Async XLA Ops:
  1.5 37.4 %copy-start.9 = (bf16[1,4,8,8,128]{4,3,2,1,0:T(8,128)(2,1)S(1)}, bf16[1,4,8,8,128]{4,3,2,1,0:T(8,128)(2,1)}, u32[]{:S(2)}) copy-start(bf16[1,4,8,8,128]{4,3,2,1,0:T(8,128)(2,1)} %param.5) | copy-start | bytes 196612
  1.5 37.4 %copy-start.10 = (bf16[1,4,8,8,128]{4,3,2,1,0:T(8,128)(2,1)S(1)}, bf16[1,4,8,8,128]{4,3,2,1,0:T(8,128)(2,1)}, u32[]{:S(2)}) copy-start(bf16[1,4,8,8,128]{4,3,2,1,0:T(8,128)(2,1)} %param.4) | copy-start | bytes 196612
  37.0 38.8 %copy-start = (bf16[32,112,128]{2,1,0:T(8,128)(2,1)}, bf16[32,112,128]{2,1,0:T(8,128)(2,1)S(1)}, u32[]{:S(2)}) copy-start(bf16[32,112,128]{2,1,0:T(8,128)(2,1)S(1)} %all_to_all.15.refs_8_) | copy-start | bytes 2752516
  37.0 38.8 %collective-permute-start.7 = (bf16[32,112,128]{2,1,0:T(8,128)(2,1)S(1)}, bf16[32,112,128]{2,1,0:T(8,128)(2,1)}, u32[]{:S(2)}, u32[]{:S(2)}) collective-permute-start(bf16[32,112,128]{2,1,0:T(8,128)(2,1)S(1)} %all_to_all.15.refs_8_), channel_id=1, source_target_pairs={{0,8},{8,0},{1,9},{9,1},{2,10},{10,2},{3,11},{11,3},{4,12},{12,4},... | collective-permute-start | bytes 2752520 | tf_op jit(solution)/shard_map/ppermute | solution.py:470
  38.9 36.9 %copy-start.1 = (bf16[512,128]{1,0:T(8,128)(2,1)}, bf16[512,128]{1,0:T(8,128)(2,1)S(1)}, u32[]{:S(2)}) copy-start(bf16[512,128]{1,0:T(8,128)(2,1)S(1)} %pad_maximum_fusion.refs_0_) | copy-start | bytes 393220
  38.9 15.1 %collective-permute-start.1 = (bf16[512,128]{1,0:T(8,128)(2,1)S(1)}, bf16[512,128]{1,0:T(8,128)(2,1)S(1)}, u32[]{:S(2)}, u32[]{:S(2)}) collective-permute-start(bf16[512,128]{1,0:T(8,128)(2,1)S(1)} %pad_maximum_fusion.refs_0_), channel_id=1, source_target_pairs={{7,0},{0,1},{1,2},{2,3},{3,4},{4,5},{5,6},{6,7},{15,8},{8,9},{9,10... | collective-permute-start | bytes 393224 | tf_op jit(solution)/shard_map/ppermute | solution.py:443
  43.2 12.7 %collective-permute-start = (bf16[512,128]{1,0:T(8,128)(2,1)S(1)}, bf16[512,128]{1,0:T(8,128)(2,1)S(1)}, u32[]{:S(2)}, u32[]{:S(2)}) collective-permute-start(bf16[512,128]{1,0:T(8,128)(2,1)S(1)} %pad_maximum_fusion.refs_0_), channel_id=1, source_target_pairs={{1,0},{2,1},{3,2},{4,3},{5,4},{6,5},{7,6},{0,7},{9,8},{10,9},{11,1... | collective-permute-start | bytes 393224 | tf_op jit(solution)/shard_map/ppermute | solution.py:443
  54.0 21.8 %copy-start.2 = (bf16[512,128]{1,0:T(8,128)(2,1)}, bf16[512,128]{1,0:T(8,128)(2,1)S(1)}, u32[]{:S(2)}) copy-start(bf16[512,128]{1,0:T(8,128)(2,1)S(1)} %collective-permute-done.1.refs_2_) | copy-start | bytes 393220
  54.0 11.9 %collective-permute-start.3 = (bf16[512,128]{1,0:T(8,128)(2,1)S(1)}, bf16[512,128]{1,0:T(8,128)(2,1)S(1)}, u32[]{:S(2)}, u32[]{:S(2)}) collective-permute-start(bf16[512,128]{1,0:T(8,128)(2,1)S(1)} %collective-permute-done.1.refs_2_), channel_id=1, source_target_pairs={{7,0},{0,1},{1,2},{2,3},{3,4},{4,5},{5,6},{6,7},{15,8},{8,9},{9,10... | collective-permute-start | bytes 393224 | tf_op jit(solution)/shard_map/ppermute | solution.py:443
  56.0 19.8 %copy-start.3 = (bf16[512,128]{1,0:T(8,128)(2,1)}, bf16[512,128]{1,0:T(8,128)(2,1)S(1)}, u32[]{:S(2)}) copy-start(bf16[512,128]{1,0:T(8,128)(2,1)S(1)} %collective-permute-done.refs_1_) | copy-start | bytes 393220
  56.0 11.9 %collective-permute-start.2 = (bf16[512,128]{1,0:T(8,128)(2,1)S(1)}, bf16[512,128]{1,0:T(8,128)(2,1)S(1)}, u32[]{:S(2)}, u32[]{:S(2)}) collective-permute-start(bf16[512,128]{1,0:T(8,128)(2,1)S(1)} %collective-permute-done.refs_1_), channel_id=1, source_target_pairs={{1,0},{2,1},{3,2},{4,3},{5,4},{6,5},{7,6},{0,7},{9,8},{10,9},{11,1... | collective-permute-start | bytes 393224 | tf_op jit(solution)/shard_map/ppermute | solution.py:443
  61.1 13.6 %collective-permute-start.6 = (bf16[512,128]{1,0:T(8,128)(2,1)S(1)}, bf16[512,128]{1,0:T(8,128)(2,1)S(1)}, u32[]{:S(2)}, u32[]{:S(2)}) collective-permute-start(bf16[512,128]{1,0:T(8,128)(2,1)S(1)} %pad_maximum_fusion.refs_0_), channel_id=1, source_target_pairs={{4,0},{5,1},{6,2},{7,3},{0,4},{1,5},{2,6},{3,7},{12,8},{13,9},{14,... | collective-permute-start | bytes 393224 | tf_op jit(solution)/shard_map/ppermute | solution.py:443
  65.9 9.9 %copy-start.4 = (bf16[512,128]{1,0:T(8,128)(2,1)}, bf16[512,128]{1,0:T(8,128)(2,1)S(1)}, u32[]{:S(2)}) copy-start(bf16[512,128]{1,0:T(8,128)(2,1)S(1)} %collective-permute-done.3.refs_4_) | copy-start | bytes 393220
  66.0 9.8 %collective-permute-start.5 = (bf16[512,128]{1,0:T(8,128)(2,1)S(1)}, bf16[512,128]{1,0:T(8,128)(2,1)S(1)}, u32[]{:S(2)}, u32[]{:S(2)}) collective-permute-start(bf16[512,128]{1,0:T(8,128)(2,1)S(1)} %collective-permute-done.3.refs_4_), channel_id=1, source_target_pairs={{7,0},{0,1},{1,2},{2,3},{3,4},{4,5},{5,6},{6,7},{15,8},{8,9},{9,10... | collective-permute-start | bytes 393224 | tf_op jit(solution)/shard_map/ppermute | solution.py:443
  67.9 7.9 %copy-start.5 = (bf16[512,128]{1,0:T(8,128)(2,1)}, bf16[512,128]{1,0:T(8,128)(2,1)S(1)}, u32[]{:S(2)}) copy-start(bf16[512,128]{1,0:T(8,128)(2,1)S(1)} %collective-permute-done.2.refs_3_) | copy-start | bytes 393220
  67.9 7.9 %collective-permute-start.4 = (bf16[512,128]{1,0:T(8,128)(2,1)S(1)}, bf16[512,128]{1,0:T(8,128)(2,1)S(1)}, u32[]{:S(2)}, u32[]{:S(2)}) collective-permute-start(bf16[512,128]{1,0:T(8,128)(2,1)S(1)} %collective-permute-done.2.refs_3_), channel_id=1, source_target_pairs={{1,0},{2,1},{3,2},{4,3},{5,4},{6,5},{7,6},{0,7},{9,8},{10,9},{11,1... | collective-permute-start | bytes 393224 | tf_op jit(solution)/shard_map/ppermute | solution.py:443
  74.7 1.2 copy-start.6
  75.7 0.7 copy-start.7
  75.8 0.7 copy-start.8
  110.2 21.2 %all-to-all-start.2 = ((bf16[64,16,128]{2,1,0:T(8,128)(2,1)}), bf16[64,16,128]{2,1,0:T(8,128)(2,1)S(1)}, u32[]{:S(2)}, u32[]{:S(2)}) async-start(bf16[64,16,128]{2,1,0:T(8,128)(2,1)} %bitcast.6), calls=%async_computation.2 | async-start | bytes 524288 | tf_op jit(solution)/shard_map/all_to_all | solution.py:478

commit v3 on v2

--- a/solution.py
+++ b/solution.py
@@ -396,11 +396,29 @@
 
 
 def near_kernel(parts, out):
-    out[...] = jnp.sum(parts[...].astype(f32), axis=0).astype(bf16)
-
-
-def near_call(parts):
-    return call(near_kernel, [(parts.shape[1:], bf16)], [], parts)[0]
+    total = jnp.sum(parts[...].astype(f32), axis=0).astype(bf16)
+    far = parts.shape[1]
+    copies = out.shape[0] // far
+    for y in range(far):
+        for n in range(copies):
+            out[y * copies + n] = total[y]
+
+
+def near_call(parts, copies):
+    shape = (parts.shape[1] * copies,) + parts.shape[2:]
+    return call(near_kernel, [(shape, bf16)], [], parts)[0]
+
+
+def copies_kernel(first, second, out):
+    part, padded = first.shape[0], out.shape[1] // 2
+    gap = jnp.zeros((padded - part, C), bf16)
+    rows = jnp.concatenate([first[...], gap, second[...], gap])
+    for n in range(out.shape[0]):
+        out[n] = rows
+
+
+def copies_call(first, second, count, padded):
+    return call(copies_kernel, [((count, 2 * padded, C), bf16)], [], first, second)[0]
 
 
 def far_kernel(factor, parts, first, second):
@@ -422,20 +440,15 @@
     )
 
 
-def spread(x, axes, count):
-    copies = jnp.broadcast_to(x[None], (count,) + x.shape)
-    return lax.all_to_all(copies, axes, 0, 0, tiled=True)
-
-
 def solution(mesh):
     dp, space = mesh.shape["dp"], mesh.shape["space"]
     across = 4
     fine = Mesh(
-        mesh.devices.reshape(dp // (2 * across), across, 2, space),
-        ("y", "x", "core", "space"),
+        mesh.devices.reshape(dp // (4 * across), 2, across, 2, space),
+        ("pair", "y", "x", "core", "space"),
     )
     swap = [(0, 1), (1, 0)]
-    near = 2 * across
+    near = 4 * across
     far = dp // near
 
     def shifted(x, hops):
@@ -462,22 +475,20 @@
         core = lax.axis_index("core")
         place = jnp.stack([lax.axis_index("space"), core]).astype(jnp.int32)
 
-        tall = ((0, padded - part), (0, 0))
-        shard = jnp.concatenate([jnp.pad(first_weight, tall), jnp.pad(second_weight, tall)])
-        mine = spread(shard, ("y", "x"), far * across)
+        mine = lax.all_to_all(
+            copies_call(first_weight, second_weight, dp // 2, padded),
+            ("pair", "y", "x"), 0, 0, tiled=True,
+        )
         pair = jnp.concatenate([image.reshape(slab, C), cotangent.reshape(slab, C)])
         blocks = whole_patch(pair)
         theirs = lax.ppermute(mine, "core", swap)
         output, outer_slab, first_delta, grads, w1 = main_call(
             place, blocks, mine, theirs, slab, chunks
         )
-        parts = lax.all_to_all(grads, ("x", "core"), 0, 0, tiled=True)
+        parts = lax.all_to_all(grads, ("y", "x", "core"), 0, 0, tiled=True)
         image_grad = fourth_call(place, first_delta, w1, outer_slab)
-        sums = near_call(parts)
-        spaced = jnp.broadcast_to(sums[:, None], (far, space) + sums.shape[1:])
-        ends = lax.all_to_all(
-            spaced.reshape((far * space,) + sums.shape[1:]), ("y", "space"), 0, 0, tiled=True
-        )
+        sums = near_call(parts, space)
+        ends = lax.all_to_all(sums, ("pair", "space"), 0, 0, tiled=True)
         first_grad, second_grad = far_call(
             ends.reshape((far, space) + sums.shape[1:]), part, factor
         )
@@ -488,7 +499,7 @@
             second_grad,
         )
 
-    dp_axes = ("y", "x", "core")
+    dp_axes = ("pair", "y", "x", "core")
     field = P(dp_axes, "space", None, None, None)
     rows = P(dp_axes, None)
     return jax.shard_map(

time: 133 us -> 133 us (level)
  the two profiles are of different devices: /device:TPU:2 before, /device:TPU:8 now
where the time goes in v3:
time: 133 us; the launch traced here: 132 us
  blocking collectives  46.8 us (35%)
  starting transfers between devices  39.4 us (30%)
  Pallas kernels  25.9 us (19%)
  waiting for transfers between devices  15.6 us (12%)
  local copies, waits for them, and re-layouts  3.68 us (3%)
    all_to_all x1, blocking collectives, step(): lax.all_to_all(copies_call(first_weight, second_weight, dp // 2, padded),...  34.6 us
    ppermute x7, starting transfers between devices, shifted(): return lax.ppermute(x, 'space', pairs)  31.8 us
    pallas_call x5, Pallas kernels, call(): pl.pallas_call(kernel, out_shape=tuple((jax.ShapeDtypeStruct(s, d) for s,...  25.9 us
    all_to_all x1, blocking collectives, step(): parts = lax.all_to_all(grads, ('y', 'x', 'core'), 0, 0, tiled=True)  12.1 us
    all_to_all x1, waiting for transfers between devices, step(): ends = lax.all_to_all(sums, ('pair', 'space'), 0, 0, tiled=True)  10.7 us
    all_to_all x1, starting transfers between devices, step(): ends = lax.all_to_all(sums, ('pair', 'space'), 0, 0, tiled=True)  5.73 us
    ppermute x7, waiting for transfers between devices, shifted(): return lax.ppermute(x, 'space', pairs)  4.84 us
    unnamed x28, local copies, waits for them, and re-layouts  3.68 us
  transfers between devices with their start and end apart: 9, of which 4 were waited for; matrix products, arithmetic and copies ran while one was open for 0% of the time, Pallas kernels for 2%

profile of v3, /device:TPU:8, one launch (start us, length us, event | category | flops | bytes accessed | tf_op | source)
XLA Modules:
  0.0 132.3 jit_solution(708966232293441357)
XLA Ops:
  0.6 0.0 copy-start
  0.6 0.7 copy-done
  1.3 0.0 copy-start.1
  1.3 0.7 copy-done.1
  2.1 0.1 shard_map.75
  2.2 0.0 copy-start.12
  2.2 0.0 copy-start.13
  2.2 34.6 %all_to_all.15.refs_8_ = bf16[32,112,128]{2,1,0:T(8,128)(2,1)S(1)} all-to-all(bf16[32,112,128]{2,1,0:T(8,128)(2,1)S(1)} %shard_map.75), channel_id=1, replica_groups=mesh['pair'=4,'y'=2,'x'=4,'core'=2,'space'=8] {'pair','y','x'}, dimensions={0} | all-to-all | bytes 1835008 | tf_op jit(solution)/shard_map/all_to_all | solution.py:478
  36.9 0.0 copy-start.2
  36.9 1.9 %collective-permute-start.7 = (bf16[32,112,128]{2,1,0:T(8,128)(2,1)S(1)}, bf16[32,112,128]{2,1,0:T(8,128)(2,1)S(1)}, u32[]{:S(2)}, u32[]{:S(2)}) collective-permute-start(bf16[32,112,128]{2,1,0:T(8,128)(2,1)S(1)} %all_to_all.15.refs_8_), channel_id=1, source_target_pairs={{0,8},{8,0},{1,9},{9,1},{2,10},{10,2},{3,11},{11,3},{4,12},{12,4},... | collective-permute-start | bytes 2752520 | tf_op jit(solution)/shard_map/ppermute | solution.py:484
  38.8 0.0 copy-done.12
  38.8 0.0 copy-done.13
  38.8 0.0 copy-start.4
  38.8 4.3 %collective-permute-start.1 = (bf16[512,128]{1,0:T(8,128)(2,1)S(1)}, bf16[512,128]{1,0:T(8,128)(2,1)S(1)}, u32[]{:S(2)}, u32[]{:S(2)}) collective-permute-start(bf16[512,128]{1,0:T(8,128)(2,1)S(1)} %pad_maximum_fusion.refs_0_), channel_id=1, source_target_pairs={{7,0},{0,1},{1,2},{2,3},{3,4},{4,5},{5,6},{6,7},{15,8},{8,9},{9,10... | collective-permute-start | bytes 393224 | tf_op jit(solution)/shard_map/ppermute | solution.py:456
  43.1 8.6 %collective-permute-start = (bf16[512,128]{1,0:T(8,128)(2,1)S(1)}, bf16[512,128]{1,0:T(8,128)(2,1)S(1)}, u32[]{:S(2)}, u32[]{:S(2)}) collective-permute-start(bf16[512,128]{1,0:T(8,128)(2,1)S(1)} %pad_maximum_fusion.refs_0_), channel_id=1, source_target_pairs={{1,0},{2,1},{3,2},{4,3},{5,4},{6,5},{7,6},{0,7},{9,8},{10,9},{11,1... | collective-permute-start | bytes 393224 | tf_op jit(solution)/shard_map/ppermute | solution.py:456
  51.7 2.2 %collective-permute-done.1.refs_2_ = bf16[512,128]{1,0:T(8,128)(2,1)S(1)} collective-permute-done((bf16[512,128]{1,0:T(8,128)(2,1)S(1)}, bf16[512,128]{1,0:T(8,128)(2,1)S(1)}, u32[]{:S(2)}, u32[]{:S(2)}) %collective-permute-start.1) | collective-permute-done | bytes 131104 | tf_op jit(solution)/shard_map/ppermute | solution.py:456
  53.9 0.0 copy-start.5
  53.9 1.9 %collective-permute-start.3 = (bf16[512,128]{1,0:T(8,128)(2,1)S(1)}, bf16[512,128]{1,0:T(8,128)(2,1)S(1)}, u32[]{:S(2)}, u32[]{:S(2)}) collective-permute-start(bf16[512,128]{1,0:T(8,128)(2,1)S(1)} %collective-permute-done.1.refs_2_), channel_id=1, source_target_pairs={{7,0},{0,1},{1,2},{2,3},{3,4},{4,5},{5,6},{6,7},{15,8},{8,9},{9,10... | collective-permute-start | bytes 393224 | tf_op jit(solution)/shard_map/ppermute | solution.py:456
  55.8 0.0 collective-permute-done.refs_1_
  55.9 0.0 copy-start.6
  55.9 5.1 %collective-permute-start.2 = (bf16[512,128]{1,0:T(8,128)(2,1)S(1)}, bf16[512,128]{1,0:T(8,128)(2,1)S(1)}, u32[]{:S(2)}, u32[]{:S(2)}) collective-permute-start(bf16[512,128]{1,0:T(8,128)(2,1)S(1)} %collective-permute-done.refs_1_), channel_id=1, source_target_pairs={{1,0},{2,1},{3,2},{4,3},{5,4},{6,5},{7,6},{0,7},{9,8},{10,9},{11,1... | collective-permute-start | bytes 393224 | tf_op jit(solution)/shard_map/ppermute | solution.py:456
  61.0 4.8 %collective-permute-start.6 = (bf16[512,128]{1,0:T(8,128)(2,1)S(1)}, bf16[512,128]{1,0:T(8,128)(2,1)S(1)}, u32[]{:S(2)}, u32[]{:S(2)}) collective-permute-start(bf16[512,128]{1,0:T(8,128)(2,1)S(1)} %pad_maximum_fusion.refs_0_), channel_id=1, source_target_pairs={{4,0},{5,1},{6,2},{7,3},{0,4},{1,5},{2,6},{3,7},{12,8},{13,9},{14,... | collective-permute-start | bytes 393224 | tf_op jit(solution)/shard_map/ppermute | solution.py:456
  65.8 0.0 collective-permute-done.3.refs_4_
  65.8 0.0 copy-done.6
  65.9 0.0 copy-start.7
  65.9 1.9 %collective-permute-start.5 = (bf16[512,128]{1,0:T(8,128)(2,1)S(1)}, bf16[512,128]{1,0:T(8,128)(2,1)S(1)}, u32[]{:S(2)}, u32[]{:S(2)}) collective-permute-start(bf16[512,128]{1,0:T(8,128)(2,1)S(1)} %collective-permute-done.3.refs_4_), channel_id=1, source_target_pairs={{7,0},{0,1},{1,2},{2,3},{3,4},{4,5},{5,6},{6,7},{15,8},{8,9},{9,10... | collective-permute-start | bytes 393224 | tf_op jit(solution)/shard_map/ppermute | solution.py:456
  67.8 0.0 collective-permute-done.2.refs_3_
  67.8 0.0 copy-start.8
  67.8 5.1 %collective-permute-start.4 = (bf16[512,128]{1,0:T(8,128)(2,1)S(1)}, bf16[512,128]{1,0:T(8,128)(2,1)S(1)}, u32[]{:S(2)}, u32[]{:S(2)}) collective-permute-start(bf16[512,128]{1,0:T(8,128)(2,1)S(1)} %collective-permute-done.2.refs_3_), channel_id=1, source_target_pairs={{1,0},{2,1},{3,2},{4,3},{5,4},{6,5},{7,6},{0,7},{9,8},{10,9},{11,1... | collective-permute-start | bytes 393224 | tf_op jit(solution)/shard_map/ppermute | solution.py:456
  73.0 0.1 pad_add_fusion.place
  73.0 1.5 %collective-permute-done.6.refs_7_ = bf16[512,128]{1,0:T(8,128)(2,1)S(1)} collective-permute-done((bf16[512,128]{1,0:T(8,128)(2,1)S(1)}, bf16[512,128]{1,0:T(8,128)(2,1)S(1)}, u32[]{:S(2)}, u32[]{:S(2)}) %collective-permute-start.6) | collective-permute-done | bytes 131104 | tf_op jit(solution)/shard_map/ppermute | solution.py:456
  74.6 0.0 copy-start.9
  74.6 1.1 collective-permute-done.5.refs_6_
  75.6 0.0 copy-start.10
  75.6 0.0 collective-permute-done.4.refs_5_
  75.7 0.0 copy-done.5
  75.7 0.0 copy-done.7
  75.7 0.0 copy-done.8
  75.7 0.0 copy-done.9
  75.7 0.6 copy-done.10
  76.3 0.0 copy-start.11
  76.3 0.6 copy-done.11
  76.9 0.0 collective-permute-done.7.refs_9_
  77.0 0.0 copy-done.2
  77.0 0.0 copy-done.4
  77.0 0.0 copy-start.3
  77.0 1.0 copy-done.3
  77.9 22.3 %shard_map.76 = (bf16[256,128]{1,0:T(8,128)(2,1)}, f32[256,128]{1,0:T(8,128)S(1)}, bf16[2048,128]{1,0:T(8,128)(2,1)S(1)}, bf16[16,4,16,128]{3,2,1,0:T(8,128)(2,1)S(1)}, bf16[384,1152]{1,0:T(8,128)(2,1)S(1)}) custom-call(s32[2]{0:T(128)S(1)} %pad_add_fusion.place, bf16[512,128]{1,0:T(8,128)(2,1)} %copy-done.4, bf16[512,128]{1,0:T(8,128)(2,1)} %copy-done.6, ...), custom_call_target="tpu_custom_call" | custom-call | tf_op jit(solution)/shard_map/pallas_call | solution.py:341
  100.2 12.1 %all_to_all.16.parts = bf16[16,4,16,128]{3,2,1,0:T(8,128)(2,1)S(1)} all-to-all(bf16[16,4,16,128]{3,2,1,0:T(8,128)(2,1)S(1)} %get-tuple-element.15), channel_id=1, replica_groups=mesh['pair'=4,'y'=2,'x'=4,'core'=2,'space'=8] {'y','x','core'}, dimensions={0} | all-to-all | bytes 524288 | tf_op jit(solution)/shard_map/all_to_all | solution.py:488
  112.3 0.7 shard_map.78
  113.0 5.7 %all-to-all-start.2 = ((bf16[32,16,128]{2,1,0:T(8,128)(2,1)}), bf16[32,16,128]{2,1,0:T(8,128)(2,1)S(1)}, u32[]{:S(2)}, u32[]{:S(2)}) async-start(bf16[32,16,128]{2,1,0:T(8,128)(2,1)} %shard_map.78), calls=%async_computation.2 | async-start | bytes 262144 | tf_op jit(solution)/shard_map/all_to_all | solution.py:491
  118.8 2.1 %shard_map.77 = bf16[256,128]{1,0:T(8,128)(2,1)} custom-call(s32[2]{0:T(128)S(1)} %pad_add_fusion.place, bf16[2048,128]{1,0:T(8,128)(2,1)S(1)} %get-tuple-element.12.delta, bf16[384,1152]{1,0:T(8,128)(2,1)S(1)} %get-tuple-element.13.weight, f32[256,128]{1,0:T(8,128)S(1)} %get-tuple-element.14.outer_slab), custom_call_target="tpu_custom_call" | custom-call | tf_op jit(solution)/shard_map/pallas_call | solution.py:341
  120.9 10.7 %all-to-all-done.2 = bf16[32,16,128]{2,1,0:T(8,128)(2,1)S(1)} async-done(((bf16[32,16,128]{2,1,0:T(8,128)(2,1)}), bf16[32,16,128]{2,1,0:T(8,128)(2,1)S(1)}, u32[]{:S(2)}, u32[]{:S(2)}) %all-to-all-start.2) | async-done | bytes 131104 | tf_op jit(solution)/shard_map/all_to_all | solution.py:491
  131.6 0.6 shard_map.79
  (1 shorter events, 0.0 us)
Async XLA Ops:
  0.6 0.7 copy-start
  1.3 0.7 copy-start.1
  2.2 36.6 %copy-start.12 = (bf16[1,4,8,8,128]{4,3,2,1,0:T(8,128)(2,1)S(1)}, bf16[1,4,8,8,128]{4,3,2,1,0:T(8,128)(2,1)}, u32[]{:S(2)}) copy-start(bf16[1,4,8,8,128]{4,3,2,1,0:T(8,128)(2,1)} %param.5) | copy-start | bytes 196612
  2.2 36.6 %copy-start.13 = (bf16[1,4,8,8,128]{4,3,2,1,0:T(8,128)(2,1)S(1)}, bf16[1,4,8,8,128]{4,3,2,1,0:T(8,128)(2,1)}, u32[]{:S(2)}) copy-start(bf16[1,4,8,8,128]{4,3,2,1,0:T(8,128)(2,1)} %param.4) | copy-start | bytes 196612
  36.9 40.1 %copy-start.2 = (bf16[32,112,128]{2,1,0:T(8,128)(2,1)}, bf16[32,112,128]{2,1,0:T(8,128)(2,1)S(1)}, u32[]{:S(2)}) copy-start(bf16[32,112,128]{2,1,0:T(8,128)(2,1)S(1)} %all_to_all.15.refs_8_) | copy-start | bytes 2752516
  36.9 40.1 %collective-permute-start.7 = (bf16[32,112,128]{2,1,0:T(8,128)(2,1)S(1)}, bf16[32,112,128]{2,1,0:T(8,128)(2,1)S(1)}, u32[]{:S(2)}, u32[]{:S(2)}) collective-permute-start(bf16[32,112,128]{2,1,0:T(8,128)(2,1)S(1)} %all_to_all.15.refs_8_), channel_id=1, source_target_pairs={{0,8},{8,0},{1,9},{9,1},{2,10},{10,2},{3,11},{11,3},{4,12},{12,4},... | collective-permute-start | bytes 2752520 | tf_op jit(solution)/shard_map/ppermute | solution.py:484
  38.8 38.1 %copy-start.4 = (bf16[512,128]{1,0:T(8,128)(2,1)}, bf16[512,128]{1,0:T(8,128)(2,1)S(1)}, u32[]{:S(2)}) copy-start(bf16[512,128]{1,0:T(8,128)(2,1)S(1)} %pad_maximum_fusion.refs_0_) | copy-start | bytes 393220
  38.8 15.1 %collective-permute-start.1 = (bf16[512,128]{1,0:T(8,128)(2,1)S(1)}, bf16[512,128]{1,0:T(8,128)(2,1)S(1)}, u32[]{:S(2)}, u32[]{:S(2)}) collective-permute-start(bf16[512,128]{1,0:T(8,128)(2,1)S(1)} %pad_maximum_fusion.refs_0_), channel_id=1, source_target_pairs={{7,0},{0,1},{1,2},{2,3},{3,4},{4,5},{5,6},{6,7},{15,8},{8,9},{9,10... | collective-permute-start | bytes 393224 | tf_op jit(solution)/shard_map/ppermute | solution.py:456
  43.1 12.7 %collective-permute-start = (bf16[512,128]{1,0:T(8,128)(2,1)S(1)}, bf16[512,128]{1,0:T(8,128)(2,1)S(1)}, u32[]{:S(2)}, u32[]{:S(2)}) collective-permute-start(bf16[512,128]{1,0:T(8,128)(2,1)S(1)} %pad_maximum_fusion.refs_0_), channel_id=1, source_target_pairs={{1,0},{2,1},{3,2},{4,3},{5,4},{6,5},{7,6},{0,7},{9,8},{10,9},{11,1... | collective-permute-start | bytes 393224 | tf_op jit(solution)/shard_map/ppermute | solution.py:456
  53.9 21.7 %copy-start.5 = (bf16[512,128]{1,0:T(8,128)(2,1)}, bf16[512,128]{1,0:T(8,128)(2,1)S(1)}, u32[]{:S(2)}) copy-start(bf16[512,128]{1,0:T(8,128)(2,1)S(1)} %collective-permute-done.1.refs_2_) | copy-start | bytes 393220
  53.9 11.9 %collective-permute-start.3 = (bf16[512,128]{1,0:T(8,128)(2,1)S(1)}, bf16[512,128]{1,0:T(8,128)(2,1)S(1)}, u32[]{:S(2)}, u32[]{:S(2)}) collective-permute-start(bf16[512,128]{1,0:T(8,128)(2,1)S(1)} %collective-permute-done.1.refs_2_), channel_id=1, source_target_pairs={{7,0},{0,1},{1,2},{2,3},{3,4},{4,5},{5,6},{6,7},{15,8},{8,9},{9,10... | collective-permute-start | bytes 393224 | tf_op jit(solution)/shard_map/ppermute | solution.py:456
  55.9 10.0 %copy-start.6 = (bf16[512,128]{1,0:T(8,128)(2,1)}, bf16[512,128]{1,0:T(8,128)(2,1)S(1)}, u32[]{:S(2)}) copy-start(bf16[512,128]{1,0:T(8,128)(2,1)S(1)} %collective-permute-done.refs_1_) | copy-start | bytes 393220
  55.9 11.9 %collective-permute-start.2 = (bf16[512,128]{1,0:T(8,128)(2,1)S(1)}, bf16[512,128]{1,0:T(8,128)(2,1)S(1)}, u32[]{:S(2)}, u32[]{:S(2)}) collective-permute-start(bf16[512,128]{1,0:T(8,128)(2,1)S(1)} %collective-permute-done.refs_1_), channel_id=1, source_target_pairs={{1,0},{2,1},{3,2},{4,3},{5,4},{6,5},{7,6},{0,7},{9,8},{10,9},{11,1... | collective-permute-start | bytes 393224 | tf_op jit(solution)/shard_map/ppermute | solution.py:456
  61.0 13.6 %collective-permute-start.6 = (bf16[512,128]{1,0:T(8,128)(2,1)S(1)}, bf16[512,128]{1,0:T(8,128)(2,1)S(1)}, u32[]{:S(2)}, u32[]{:S(2)}) collective-permute-start(bf16[512,128]{1,0:T(8,128)(2,1)S(1)} %pad_maximum_fusion.refs_0_), channel_id=1, source_target_pairs={{4,0},{5,1},{6,2},{7,3},{0,4},{1,5},{2,6},{3,7},{12,8},{13,9},{14,... | collective-permute-start | bytes 393224 | tf_op jit(solution)/shard_map/ppermute | solution.py:456
  65.9 9.8 %copy-start.7 = (bf16[512,128]{1,0:T(8,128)(2,1)}, bf16[512,128]{1,0:T(8,128)(2,1)S(1)}, u32[]{:S(2)}) copy-start(bf16[512,128]{1,0:T(8,128)(2,1)S(1)} %collective-permute-done.3.refs_4_) | copy-start | bytes 393220
  65.9 9.8 %collective-permute-start.5 = (bf16[512,128]{1,0:T(8,128)(2,1)S(1)}, bf16[512,128]{1,0:T(8,128)(2,1)S(1)}, u32[]{:S(2)}, u32[]{:S(2)}) collective-permute-start(bf16[512,128]{1,0:T(8,128)(2,1)S(1)} %collective-permute-done.3.refs_4_), channel_id=1, source_target_pairs={{7,0},{0,1},{1,2},{2,3},{3,4},{4,5},{5,6},{6,7},{15,8},{8,9},{9,10... | collective-permute-start | bytes 393224 | tf_op jit(solution)/shard_map/ppermute | solution.py:456
  67.8 7.9 %copy-start.8 = (bf16[512,128]{1,0:T(8,128)(2,1)}, bf16[512,128]{1,0:T(8,128)(2,1)S(1)}, u32[]{:S(2)}) copy-start(bf16[512,128]{1,0:T(8,128)(2,1)S(1)} %collective-permute-done.2.refs_3_) | copy-start | bytes 393220
  67.8 7.8 %collective-permute-start.4 = (bf16[512,128]{1,0:T(8,128)(2,1)S(1)}, bf16[512,128]{1,0:T(8,128)(2,1)S(1)}, u32[]{:S(2)}, u32[]{:S(2)}) collective-permute-start(bf16[512,128]{1,0:T(8,128)(2,1)S(1)} %collective-permute-done.2.refs_3_), channel_id=1, source_target_pairs={{1,0},{2,1},{3,2},{4,3},{5,4},{6,5},{7,6},{0,7},{9,8},{10,9},{11,1... | collective-permute-start | bytes 393224 | tf_op jit(solution)/shard_map/ppermute | solution.py:456
  74.6 1.1 copy-start.9
  75.6 0.7 copy-start.10
  76.3 0.7 copy-start.11
  77.0 1.0 copy-start.3
  113.0 18.6 %all-to-all-start.2 = ((bf16[32,16,128]{2,1,0:T(8,128)(2,1)}), bf16[32,16,128]{2,1,0:T(8,128)(2,1)S(1)}, u32[]{:S(2)}, u32[]{:S(2)}) async-start(bf16[32,16,128]{2,1,0:T(8,128)(2,1)} %shard_map.78), calls=%async_computation.2 | async-start | bytes 262144 | tf_op jit(solution)/shard_map/all_to_all | solution.py:491

commit v4 on v1

--- a/solution.py
+++ b/solution.py
@@ -109,12 +109,12 @@
 
 
 def assemble(core, mine, theirs, flat, weight):
-    across, chips = mine.shape[0], mine.shape[0] * mine.shape[1]
+    chips = mine.shape[0]
     part = ROWS // (2 * chips)
     mine_first = core == 0
     for y in range(chips):
-        one = mine[y % across, y // across].astype(f32)
-        two = theirs[y % across, y // across].astype(f32)
+        one = mine[y].astype(f32)
+        two = theirs[y].astype(f32)
         even = jnp.where(mine_first, one, two)[:part]
         odd = jnp.where(mine_first, two, one)[:part]
         flat[2 * y * part : (2 * y + 1) * part, :] = even
@@ -184,7 +184,7 @@
     planes = cells // PLANE
     slab = output.shape[0]
     count = cells // slab
-    padded = mine1.shape[2]
+    padded = mine1.shape[1]
     zero = jnp.zeros((1, C), f32)
     copy = pltpu.make_async_copy
     fields = ([], [])
@@ -197,7 +197,7 @@
             copy(block.at[row + slab : row + 2 * slab], cotangent.at[at], other_sem.at[n])
         )
     weights = [
-        copy(source.at[:, :, half * padded : (half + 1) * padded], target, weight_sem.at[n])
+        copy(source.at[:, half * padded : (half + 1) * padded], target, weight_sem.at[n])
         for n, (source, half, target) in enumerate(
             ((mine, 0, mine1), (theirs, 0, theirs1), (mine, 1, mine2), (theirs, 1, theirs2))
         )
@@ -351,7 +351,7 @@
     offsets = [(o, n) for many, _ in blocks for n, o in enumerate(many)]
     arrays = [array for many, array in blocks for _ in many]
     field = (cells, C)
-    half = mine.shape[:2] + (mine.shape[2] // 2, C)
+    half = (mine.shape[0], mine.shape[1] // 2, C)
     local = pltpu.VMEM
     signal = pltpu.SemaphoreType.DMA
     return call(
@@ -392,11 +392,29 @@
 
 
 def near_kernel(parts, out):
-    out[...] = jnp.sum(parts[...].astype(f32), axis=0).astype(bf16)
-
-
-def near_call(parts):
-    return call(near_kernel, [(parts.shape[1:], bf16)], [], parts)[0]
+    total = jnp.sum(parts[...].astype(f32), axis=0).astype(bf16)
+    far = parts.shape[1]
+    copies = out.shape[0] // far
+    for y in range(far):
+        for n in range(copies):
+            out[y * copies + n] = total[y]
+
+
+def near_call(parts, copies):
+    shape = (parts.shape[1] * copies,) + parts.shape[2:]
+    return call(near_kernel, [(shape, bf16)], [], parts)[0]
+
+
+def copies_kernel(first, second, out):
+    part, padded = first.shape[0], out.shape[1] // 2
+    gap = jnp.zeros((padded - part, C), bf16)
+    rows = jnp.concatenate([first[...], gap, second[...], gap])
+    for n in range(out.shape[0]):
+        out[n] = rows
+
+
+def copies_call(first, second, count, padded):
+    return call(copies_kernel, [((count, 2 * padded, C), bf16)], [], first, second)[0]
 
 
 def far_kernel(factor, parts, first, second):
@@ -418,20 +436,15 @@
     )
 
 
-def spread(x, axes, count):
-    copies = jnp.broadcast_to(x[None], (count,) + x.shape)
-    return lax.all_to_all(copies, axes, 0, 0, tiled=True)
-
-
 def solution(mesh):
     dp, space = mesh.shape["dp"], mesh.shape["space"]
     across = 4
     fine = Mesh(
-        mesh.devices.reshape(dp // (2 * across), across, 2, space),
-        ("y", "x", "core", "space"),
+        mesh.devices.reshape(dp // (4 * across), 2, across, 2, space),
+        ("pair", "y", "x", "core", "space"),
     )
     swap = [(0, 1), (1, 0)]
-    near = 2 * across
+    near = 4 * across
     far = dp // near
 
     def shifted(x, hops):
@@ -458,23 +471,20 @@
         core = lax.axis_index("core")
         place = jnp.stack([lax.axis_index("space"), core]).astype(jnp.int32)
 
-        tall = ((0, padded - part), (0, 0))
-        shard = jnp.concatenate([jnp.pad(first_weight, tall), jnp.pad(second_weight, tall)])
-        column = spread(shard, "y", far)
-        mine = spread(column, "x", across)
+        mine = lax.all_to_all(
+            copies_call(first_weight, second_weight, dp // 2, padded),
+            ("pair", "y", "x"), 0, 0, tiled=True,
+        )
         pair = jnp.concatenate([image.reshape(slab, C), cotangent.reshape(slab, C)])
         blocks = whole_patch(pair)
         theirs = lax.ppermute(mine, "core", swap)
         output, outer_slab, first_delta, grads, w1 = main_call(
             place, blocks, mine, theirs, slab, chunks
         )
-        parts = lax.all_to_all(grads, ("x", "core"), 0, 0, tiled=True)
+        parts = lax.all_to_all(grads, ("y", "x", "core"), 0, 0, tiled=True)
         image_grad = fourth_call(place, first_delta, w1, outer_slab)
-        sums = near_call(parts)
-        spaced = jnp.broadcast_to(sums[:, None], (far, space) + sums.shape[1:])
-        ends = lax.all_to_all(
-            spaced.reshape((far * space,) + sums.shape[1:]), ("y", "space"), 0, 0, tiled=True
-        )
+        sums = near_call(parts, space)
+        ends = lax.all_to_all(sums, ("pair", "space"), 0, 0, tiled=True)
         first_grad, second_grad = far_call(
             ends.reshape((far, space) + sums.shape[1:]), part, factor
         )
@@ -485,7 +495,7 @@
             second_grad,
         )
 
-    dp_axes = ("y", "x", "core")
+    dp_axes = ("pair", "y", "x", "core")
     field = P(dp_axes, "space", None, None, None)
     rows = P(dp_axes, None)
     return jax.shard_map(

time: 130 us -> 133 us (1.023)
  the two profiles are of different devices: /device:TPU:2 before, /device:TPU:8 now
where the time goes in v4:
time: 133 us; the launch traced here: 132 us
  blocking collectives  46.8 us (35%)
  starting transfers between devices  39.4 us (30%)
  Pallas kernels  25.6 us (19%)
  waiting for transfers between devices  15.6 us (12%)
  local copies, waits for them, and re-layouts  3.68 us (3%)
    all_to_all x1, blocking collectives, step(): lax.all_to_all(copies_call(first_weight, second_weight, dp // 2, padded),...  34.6 us
    ppermute x7, starting transfers between devices, shifted(): return lax.ppermute(x, 'space', pairs)  31.8 us
    pallas_call x5, Pallas kernels, call(): pl.pallas_call(kernel, out_shape=tuple((jax.ShapeDtypeStruct(s, d) for s,...  25.6 us
    all_to_all x1, blocking collectives, step(): parts = lax.all_to_all(grads, ('y', 'x', 'core'), 0, 0, tiled=True)  12.1 us
    all_to_all x1, waiting for transfers between devices, step(): ends = lax.all_to_all(sums, ('pair', 'space'), 0, 0, tiled=True)  10.7 us
    all_to_all x1, starting transfers between devices, step(): ends = lax.all_to_all(sums, ('pair', 'space'), 0, 0, tiled=True)  5.72 us
    ppermute x7, waiting for transfers between devices, shifted(): return lax.ppermute(x, 'space', pairs)  4.84 us
    unnamed x28, local copies, waits for them, and re-layouts  3.68 us
  transfers between devices with their start and end apart: 9, of which 4 were waited for; matrix products, arithmetic and copies ran while one was open for 0% of the time, Pallas kernels for 2%

profile of v4, /device:TPU:8, one launch (start us, length us, event | category | flops | bytes accessed | tf_op | source)
XLA Modules:
  0.0 132.0 jit_solution(2913022614418310023)
XLA Ops:
  0.6 0.0 copy-start
  0.6 0.7 copy-done
  1.3 0.0 copy-start.1
  1.3 0.7 copy-done.1
  2.1 0.1 shard_map.75
  2.2 0.0 copy-start.12
  2.2 0.0 copy-start.13
  2.2 34.6 %all_to_all.15.refs_8_ = bf16[32,112,128]{2,1,0:T(8,128)(2,1)S(1)} all-to-all(bf16[32,112,128]{2,1,0:T(8,128)(2,1)S(1)} %shard_map.75), channel_id=1, replica_groups=mesh['pair'=4,'y'=2,'x'=4,'core'=2,'space'=8] {'pair','y','x'}, dimensions={0} | all-to-all | bytes 1835008 | tf_op jit(solution)/shard_map/all_to_all | solution.py:474
  36.9 0.0 copy-start.2
  36.9 1.9 %collective-permute-start.7 = (bf16[32,112,128]{2,1,0:T(8,128)(2,1)S(1)}, bf16[32,112,128]{2,1,0:T(8,128)(2,1)S(1)}, u32[]{:S(2)}, u32[]{:S(2)}) collective-permute-start(bf16[32,112,128]{2,1,0:T(8,128)(2,1)S(1)} %all_to_all.15.refs_8_), channel_id=1, source_target_pairs={{0,8},{8,0},{1,9},{9,1},{2,10},{10,2},{3,11},{11,3},{4,12},{12,4},... | collective-permute-start | bytes 2752520 | tf_op jit(solution)/shard_map/ppermute | solution.py:480
  38.8 0.0 copy-done.12
  38.8 0.0 copy-done.13
  38.8 0.0 copy-start.4
  38.8 4.3 %collective-permute-start.1 = (bf16[512,128]{1,0:T(8,128)(2,1)S(1)}, bf16[512,128]{1,0:T(8,128)(2,1)S(1)}, u32[]{:S(2)}, u32[]{:S(2)}) collective-permute-start(bf16[512,128]{1,0:T(8,128)(2,1)S(1)} %pad_maximum_fusion.refs_0_), channel_id=1, source_target_pairs={{7,0},{0,1},{1,2},{2,3},{3,4},{4,5},{5,6},{6,7},{15,8},{8,9},{9,10... | collective-permute-start | bytes 393224 | tf_op jit(solution)/shard_map/ppermute | solution.py:452
  43.1 8.6 %collective-permute-start = (bf16[512,128]{1,0:T(8,128)(2,1)S(1)}, bf16[512,128]{1,0:T(8,128)(2,1)S(1)}, u32[]{:S(2)}, u32[]{:S(2)}) collective-permute-start(bf16[512,128]{1,0:T(8,128)(2,1)S(1)} %pad_maximum_fusion.refs_0_), channel_id=1, source_target_pairs={{1,0},{2,1},{3,2},{4,3},{5,4},{6,5},{7,6},{0,7},{9,8},{10,9},{11,1... | collective-permute-start | bytes 393224 | tf_op jit(solution)/shard_map/ppermute | solution.py:452
  51.7 2.2 %collective-permute-done.1.refs_2_ = bf16[512,128]{1,0:T(8,128)(2,1)S(1)} collective-permute-done((bf16[512,128]{1,0:T(8,128)(2,1)S(1)}, bf16[512,128]{1,0:T(8,128)(2,1)S(1)}, u32[]{:S(2)}, u32[]{:S(2)}) %collective-permute-start.1) | collective-permute-done | bytes 131104 | tf_op jit(solution)/shard_map/ppermute | solution.py:452
  53.9 0.0 copy-start.5
  53.9 1.9 %collective-permute-start.3 = (bf16[512,128]{1,0:T(8,128)(2,1)S(1)}, bf16[512,128]{1,0:T(8,128)(2,1)S(1)}, u32[]{:S(2)}, u32[]{:S(2)}) collective-permute-start(bf16[512,128]{1,0:T(8,128)(2,1)S(1)} %collective-permute-done.1.refs_2_), channel_id=1, source_target_pairs={{7,0},{0,1},{1,2},{2,3},{3,4},{4,5},{5,6},{6,7},{15,8},{8,9},{9,10... | collective-permute-start | bytes 393224 | tf_op jit(solution)/shard_map/ppermute | solution.py:452
  55.8 0.0 collective-permute-done.refs_1_
  55.9 0.0 copy-start.6
  55.9 5.1 %collective-permute-start.2 = (bf16[512,128]{1,0:T(8,128)(2,1)S(1)}, bf16[512,128]{1,0:T(8,128)(2,1)S(1)}, u32[]{:S(2)}, u32[]{:S(2)}) collective-permute-start(bf16[512,128]{1,0:T(8,128)(2,1)S(1)} %collective-permute-done.refs_1_), channel_id=1, source_target_pairs={{1,0},{2,1},{3,2},{4,3},{5,4},{6,5},{7,6},{0,7},{9,8},{10,9},{11,1... | collective-permute-start | bytes 393224 | tf_op jit(solution)/shard_map/ppermute | solution.py:452
  61.0 4.8 %collective-permute-start.6 = (bf16[512,128]{1,0:T(8,128)(2,1)S(1)}, bf16[512,128]{1,0:T(8,128)(2,1)S(1)}, u32[]{:S(2)}, u32[]{:S(2)}) collective-permute-start(bf16[512,128]{1,0:T(8,128)(2,1)S(1)} %pad_maximum_fusion.refs_0_), channel_id=1, source_target_pairs={{4,0},{5,1},{6,2},{7,3},{0,4},{1,5},{2,6},{3,7},{12,8},{13,9},{14,... | collective-permute-start | bytes 393224 | tf_op jit(solution)/shard_map/ppermute | solution.py:452
  65.8 0.0 collective-permute-done.3.refs_4_
  65.8 0.0 copy-done.6
  65.9 0.0 copy-start.7
  65.9 1.9 %collective-permute-start.5 = (bf16[512,128]{1,0:T(8,128)(2,1)S(1)}, bf16[512,128]{1,0:T(8,128)(2,1)S(1)}, u32[]{:S(2)}, u32[]{:S(2)}) collective-permute-start(bf16[512,128]{1,0:T(8,128)(2,1)S(1)} %collective-permute-done.3.refs_4_), channel_id=1, source_target_pairs={{7,0},{0,1},{1,2},{2,3},{3,4},{4,5},{5,6},{6,7},{15,8},{8,9},{9,10... | collective-permute-start | bytes 393224 | tf_op jit(solution)/shard_map/ppermute | solution.py:452
  67.8 0.0 collective-permute-done.2.refs_3_
  67.8 0.0 copy-start.8
  67.8 5.1 %collective-permute-start.4 = (bf16[512,128]{1,0:T(8,128)(2,1)S(1)}, bf16[512,128]{1,0:T(8,128)(2,1)S(1)}, u32[]{:S(2)}, u32[]{:S(2)}) collective-permute-start(bf16[512,128]{1,0:T(8,128)(2,1)S(1)} %collective-permute-done.2.refs_3_), channel_id=1, source_target_pairs={{1,0},{2,1},{3,2},{4,3},{5,4},{6,5},{7,6},{0,7},{9,8},{10,9},{11,1... | collective-permute-start | bytes 393224 | tf_op jit(solution)/shard_map/ppermute | solution.py:452
  73.0 0.1 pad_add_fusion.place
  73.0 1.5 %collective-permute-done.6.refs_7_ = bf16[512,128]{1,0:T(8,128)(2,1)S(1)} collective-permute-done((bf16[512,128]{1,0:T(8,128)(2,1)S(1)}, bf16[512,128]{1,0:T(8,128)(2,1)S(1)}, u32[]{:S(2)}, u32[]{:S(2)}) %collective-permute-start.6) | collective-permute-done | bytes 131104 | tf_op jit(solution)/shard_map/ppermute | solution.py:452
  74.6 0.0 copy-start.9
  74.6 1.1 collective-permute-done.5.refs_6_
  75.6 0.0 copy-start.10
  75.6 0.0 collective-permute-done.4.refs_5_
  75.7 0.0 copy-done.5
  75.7 0.0 copy-done.7
  75.7 0.0 copy-done.8
  75.7 0.0 copy-done.9
  75.7 0.6 copy-done.10
  76.3 0.0 copy-start.11
  76.3 0.6 copy-done.11
  76.9 0.0 collective-permute-done.7.refs_9_
  77.0 0.0 copy-done.2
  77.0 0.0 copy-done.4
  77.0 0.0 copy-start.3
  77.0 1.0 copy-done.3
  77.9 22.1 %shard_map.76 = (bf16[256,128]{1,0:T(8,128)(2,1)}, f32[256,128]{1,0:T(8,128)S(1)}, bf16[2048,128]{1,0:T(8,128)(2,1)S(1)}, bf16[16,4,16,128]{3,2,1,0:T(8,128)(2,1)S(1)}, bf16[384,1152]{1,0:T(8,128)(2,1)S(1)}) custom-call(s32[2]{0:T(128)S(1)} %pad_add_fusion.place, bf16[512,128]{1,0:T(8,128)(2,1)} %copy-done.4, bf16[512,128]{1,0:T(8,128)(2,1)} %copy-done.6, ...), custom_call_target="tpu_custom_call" | custom-call | tf_op jit(solution)/shard_map/pallas_call | solution.py:338
  100.0 12.1 %all_to_all.16.parts = bf16[16,4,16,128]{3,2,1,0:T(8,128)(2,1)S(1)} all-to-all(bf16[16,4,16,128]{3,2,1,0:T(8,128)(2,1)S(1)} %get-tuple-element.15), channel_id=1, replica_groups=mesh['pair'=4,'y'=2,'x'=4,'core'=2,'space'=8] {'y','x','core'}, dimensions={0} | all-to-all | bytes 524288 | tf_op jit(solution)/shard_map/all_to_all | solution.py:484
  112.1 0.7 shard_map.78
  112.8 5.7 %all-to-all-start.2 = ((bf16[32,16,128]{2,1,0:T(8,128)(2,1)}), bf16[32,16,128]{2,1,0:T(8,128)(2,1)S(1)}, u32[]{:S(2)}, u32[]{:S(2)}) async-start(bf16[32,16,128]{2,1,0:T(8,128)(2,1)} %shard_map.78), calls=%async_computation.2 | async-start | bytes 262144 | tf_op jit(solution)/shard_map/all_to_all | solution.py:487
  118.5 2.1 %shard_map.77 = bf16[256,128]{1,0:T(8,128)(2,1)} custom-call(s32[2]{0:T(128)S(1)} %pad_add_fusion.place, bf16[2048,128]{1,0:T(8,128)(2,1)S(1)} %get-tuple-element.12.delta, bf16[384,1152]{1,0:T(8,128)(2,1)S(1)} %get-tuple-element.13.weight, f32[256,128]{1,0:T(8,128)S(1)} %get-tuple-element.14.outer_slab), custom_call_target="tpu_custom_call" | custom-call | tf_op jit(solution)/shard_map/pallas_call | solution.py:338
  120.7 10.7 %all-to-all-done.2 = bf16[32,16,128]{2,1,0:T(8,128)(2,1)S(1)} async-done(((bf16[32,16,128]{2,1,0:T(8,128)(2,1)}), bf16[32,16,128]{2,1,0:T(8,128)(2,1)S(1)}, u32[]{:S(2)}, u32[]{:S(2)}) %all-to-all-start.2) | async-done | bytes 131104 | tf_op jit(solution)/shard_map/all_to_all | solution.py:487
  131.4 0.6 shard_map.79
  (1 shorter events, 0.0 us)
Async XLA Ops:
  0.6 0.7 copy-start
  1.3 0.7 copy-start.1
  2.2 36.6 %copy-start.12 = (bf16[1,4,8,8,128]{4,3,2,1,0:T(8,128)(2,1)S(1)}, bf16[1,4,8,8,128]{4,3,2,1,0:T(8,128)(2,1)}, u32[]{:S(2)}) copy-start(bf16[1,4,8,8,128]{4,3,2,1,0:T(8,128)(2,1)} %param.5) | copy-start | bytes 196612
  2.2 36.6 %copy-start.13 = (bf16[1,4,8,8,128]{4,3,2,1,0:T(8,128)(2,1)S(1)}, bf16[1,4,8,8,128]{4,3,2,1,0:T(8,128)(2,1)}, u32[]{:S(2)}) copy-start(bf16[1,4,8,8,128]{4,3,2,1,0:T(8,128)(2,1)} %param.4) | copy-start | bytes 196612
  36.9 40.1 %copy-start.2 = (bf16[32,112,128]{2,1,0:T(8,128)(2,1)}, bf16[32,112,128]{2,1,0:T(8,128)(2,1)S(1)}, u32[]{:S(2)}) copy-start(bf16[32,112,128]{2,1,0:T(8,128)(2,1)S(1)} %all_to_all.15.refs_8_) | copy-start | bytes 2752516
  36.9 40.1 %collective-permute-start.7 = (bf16[32,112,128]{2,1,0:T(8,128)(2,1)S(1)}, bf16[32,112,128]{2,1,0:T(8,128)(2,1)S(1)}, u32[]{:S(2)}, u32[]{:S(2)}) collective-permute-start(bf16[32,112,128]{2,1,0:T(8,128)(2,1)S(1)} %all_to_all.15.refs_8_), channel_id=1, source_target_pairs={{0,8},{8,0},{1,9},{9,1},{2,10},{10,2},{3,11},{11,3},{4,12},{12,4},... | collective-permute-start | bytes 2752520 | tf_op jit(solution)/shard_map/ppermute | solution.py:480
  38.8 38.1 %copy-start.4 = (bf16[512,128]{1,0:T(8,128)(2,1)}, bf16[512,128]{1,0:T(8,128)(2,1)S(1)}, u32[]{:S(2)}) copy-start(bf16[512,128]{1,0:T(8,128)(2,1)S(1)} %pad_maximum_fusion.refs_0_) | copy-start | bytes 393220
  38.8 15.1 %collective-permute-start.1 = (bf16[512,128]{1,0:T(8,128)(2,1)S(1)}, bf16[512,128]{1,0:T(8,128)(2,1)S(1)}, u32[]{:S(2)}, u32[]{:S(2)}) collective-permute-start(bf16[512,128]{1,0:T(8,128)(2,1)S(1)} %pad_maximum_fusion.refs_0_), channel_id=1, source_target_pairs={{7,0},{0,1},{1,2},{2,3},{3,4},{4,5},{5,6},{6,7},{15,8},{8,9},{9,10... | collective-permute-start | bytes 393224 | tf_op jit(solution)/shard_map/ppermute | solution.py:452
  43.1 12.7 %collective-permute-start = (bf16[512,128]{1,0:T(8,128)(2,1)S(1)}, bf16[512,128]{1,0:T(8,128)(2,1)S(1)}, u32[]{:S(2)}, u32[]{:S(2)}) collective-permute-start(bf16[512,128]{1,0:T(8,128)(2,1)S(1)} %pad_maximum_fusion.refs_0_), channel_id=1, source_target_pairs={{1,0},{2,1},{3,2},{4,3},{5,4},{6,5},{7,6},{0,7},{9,8},{10,9},{11,1... | collective-permute-start | bytes 393224 | tf_op jit(solution)/shard_map/ppermute | solution.py:452
  53.9 21.7 %copy-start.5 = (bf16[512,128]{1,0:T(8,128)(2,1)}, bf16[512,128]{1,0:T(8,128)(2,1)S(1)}, u32[]{:S(2)}) copy-start(bf16[512,128]{1,0:T(8,128)(2,1)S(1)} %collective-permute-done.1.refs_2_) | copy-start | bytes 393220
  53.9 11.9 %collective-permute-start.3 = (bf16[512,128]{1,0:T(8,128)(2,1)S(1)}, bf16[512,128]{1,0:T(8,128)(2,1)S(1)}, u32[]{:S(2)}, u32[]{:S(2)}) collective-permute-start(bf16[512,128]{1,0:T(8,128)(2,1)S(1)} %collective-permute-done.1.refs_2_), channel_id=1, source_target_pairs={{7,0},{0,1},{1,2},{2,3},{3,4},{4,5},{5,6},{6,7},{15,8},{8,9},{9,10... | collective-permute-start | bytes 393224 | tf_op jit(solution)/shard_map/ppermute | solution.py:452
  55.9 10.0 %copy-start.6 = (bf16[512,128]{1,0:T(8,128)(2,1)}, bf16[512,128]{1,0:T(8,128)(2,1)S(1)}, u32[]{:S(2)}) copy-start(bf16[512,128]{1,0:T(8,128)(2,1)S(1)} %collective-permute-done.refs_1_) | copy-start | bytes 393220
  55.9 11.9 %collective-permute-start.2 = (bf16[512,128]{1,0:T(8,128)(2,1)S(1)}, bf16[512,128]{1,0:T(8,128)(2,1)S(1)}, u32[]{:S(2)}, u32[]{:S(2)}) collective-permute-start(bf16[512,128]{1,0:T(8,128)(2,1)S(1)} %collective-permute-done.refs_1_), channel_id=1, source_target_pairs={{1,0},{2,1},{3,2},{4,3},{5,4},{6,5},{7,6},{0,7},{9,8},{10,9},{11,1... | collective-permute-start | bytes 393224 | tf_op jit(solution)/shard_map/ppermute | solution.py:452
  61.0 13.6 %collective-permute-start.6 = (bf16[512,128]{1,0:T(8,128)(2,1)S(1)}, bf16[512,128]{1,0:T(8,128)(2,1)S(1)}, u32[]{:S(2)}, u32[]{:S(2)}) collective-permute-start(bf16[512,128]{1,0:T(8,128)(2,1)S(1)} %pad_maximum_fusion.refs_0_), channel_id=1, source_target_pairs={{4,0},{5,1},{6,2},{7,3},{0,4},{1,5},{2,6},{3,7},{12,8},{13,9},{14,... | collective-permute-start | bytes 393224 | tf_op jit(solution)/shard_map/ppermute | solution.py:452
  65.9 9.8 %copy-start.7 = (bf16[512,128]{1,0:T(8,128)(2,1)}, bf16[512,128]{1,0:T(8,128)(2,1)S(1)}, u32[]{:S(2)}) copy-start(bf16[512,128]{1,0:T(8,128)(2,1)S(1)} %collective-permute-done.3.refs_4_) | copy-start | bytes 393220
  65.9 9.8 %collective-permute-start.5 = (bf16[512,128]{1,0:T(8,128)(2,1)S(1)}, bf16[512,128]{1,0:T(8,128)(2,1)S(1)}, u32[]{:S(2)}, u32[]{:S(2)}) collective-permute-start(bf16[512,128]{1,0:T(8,128)(2,1)S(1)} %collective-permute-done.3.refs_4_), channel_id=1, source_target_pairs={{7,0},{0,1},{1,2},{2,3},{3,4},{4,5},{5,6},{6,7},{15,8},{8,9},{9,10... | collective-permute-start | bytes 393224 | tf_op jit(solution)/shard_map/ppermute | solution.py:452
  67.8 7.9 %copy-start.8 = (bf16[512,128]{1,0:T(8,128)(2,1)}, bf16[512,128]{1,0:T(8,128)(2,1)S(1)}, u32[]{:S(2)}) copy-start(bf16[512,128]{1,0:T(8,128)(2,1)S(1)} %collective-permute-done.2.refs_3_) | copy-start | bytes 393220
  67.8 7.8 %collective-permute-start.4 = (bf16[512,128]{1,0:T(8,128)(2,1)S(1)}, bf16[512,128]{1,0:T(8,128)(2,1)S(1)}, u32[]{:S(2)}, u32[]{:S(2)}) collective-permute-start(bf16[512,128]{1,0:T(8,128)(2,1)S(1)} %collective-permute-done.2.refs_3_), channel_id=1, source_target_pairs={{1,0},{2,1},{3,2},{4,3},{5,4},{6,5},{7,6},{0,7},{9,8},{10,9},{11,1... | collective-permute-start | bytes 393224 | tf_op jit(solution)/shard_map/ppermute | solution.py:452
  74.6 1.1 copy-start.9
  75.6 0.7 copy-start.10
  76.3 0.7 copy-start.11
  77.0 1.0 copy-start.3
  112.8 18.6 %all-to-all-start.2 = ((bf16[32,16,128]{2,1,0:T(8,128)(2,1)}), bf16[32,16,128]{2,1,0:T(8,128)(2,1)S(1)}, u32[]{:S(2)}, u32[]{:S(2)}) async-start(bf16[32,16,128]{2,1,0:T(8,128)(2,1)} %shard_map.78), calls=%async_computation.2 | async-start | bytes 262144 | tf_op jit(solution)/shard_map/all_to_all | solution.py:487
